TPU v7x, 32 devices: a whole 2x2x4 slice. The times are simulated.
32 devices in a mesh: crop: 16 (over z, y, x), seq: 2 (over core).
Axes of the slice: x: 2, y: 2, z: 4, core: 2. Of those that a mesh axis runs over, the one named last changes fastest.
Arguments:
- single: bfloat16 [5120, 768], P(('crop', 'seq')), may hold values from -6 to 6
- conditioning: bfloat16 [5120, 384], P(('crop', 'seq')), may hold values from -6 to 6
- pair_features: bfloat16 [16, 320, 320, 128], P('crop', 'seq'), may hold values from -6 to 6
- segments: int32 [16, 320], P('crop'), may hold values from 0 to 3, never falling along the last dimension, each value on 1 to 160 neighbouring positions
- pad_mask: int32 [16, 320], P('crop'), may hold values from 0 to 1, as said below
- cotangent: bfloat16 [5120, 768], P(('crop', 'seq')), may hold values from -6 to 6
- cond_gain: bfloat16 [384, 2], replicated, may hold values from 0.099609375 to 1.8984375
- cond_weight: bfloat16 [384, 6, 768], replicated, may hold values from -0.3125 to 0.3125
- biases: bfloat16 [768, 5], replicated, may hold values from -3 to 3
- attn_weight: bfloat16 [768, 4, 768], replicated, may hold values from -0.21875 to 0.21875
- out_weight: bfloat16 [768, 768], replicated, may hold values from -1.75 to 1.75
- pair_gain: bfloat16 [128], replicated, may hold values from 0.099609375 to 1.8984375
- pair_weight: bfloat16 [128, 16], replicated, may hold values from -0.5 to 0.5
- expand_weight: bfloat16 [768, 2, 1536], replicated, may hold values from -0.21875 to 0.21875
- contract_weight: bfloat16 [1536, 768], replicated, may hold values from -0.15625 to 0.15625
Outputs:
- layer_out: bfloat16 [5120, 768], P(('crop', 'seq'))
- grad_single: float32 [5120, 768], P(('crop', 'seq'))
- grad_conditioning: float32 [5120, 384], P(('crop', 'seq'))
- grad_pair: bfloat16 [16, 320, 320, 128], P('crop', 'seq')
- grad_cond_gain: float32 [384, 2], P(('crop', 'seq'))
- grad_cond_weight: float32 [384, 6, 768], P(('crop', 'seq'))
- grad_biases: float32 [768, 5], P(('crop', 'seq'))
- grad_attn_weight: float32 [768, 4, 768], P(('crop', 'seq'))
- grad_out_weight: float32 [768, 768], P(('crop', 'seq'))
- grad_pair_gain: float32 [128], P(('crop', 'seq'))
- grad_pair_weight: float32 [128, 16], P(('crop', 'seq'))
- grad_expand_weight: float32 [768, 2, 1536], P(('crop', 'seq'))
- grad_contract_weight: float32 [1536, 768], P(('crop', 'seq'))
Inputs may be any that keep to these rules, and one draw needn't show every extreme that they name: `segments`: within a crop the ids never fall; a crop holds 4 documents of 1 to 160 slots each. `pad_mask`: in each crop the real tokens form a prefix of at least 240 slots; the first crop has no padding.
All inputs are finite; a program needn't handle non-finite values.
Results may differ from a plain program's by a relative error of at most 0.012.
The roundings to bfloat16 on the way count: a program that leaves them out, or rounds other values in their place, can miss the bound.
Values may be sent and summed in bfloat16 or wider, within the bound.
A program may use at most 256 MiB of HBM per device.

v0:
```python
import functools
import math
import jax
import jax.numpy as jnp
from jax import lax
from jax.experimental import pallas as pl
from jax.experimental.pallas import tpu as pltpu
from jax.sharding import PartitionSpec as P

EPS = 1e-05
NEG = -1e30
F32 = jnp.float32
BF16 = jnp.bfloat16


def dot_nt(a, b):
    return lax.dot_general(a, b, (((1,), (1,)), ((), ())), preferred_element_type=F32)


def dot_tn(a, b):
    return lax.dot_general(a, b, (((0,), (0,)), ((), ())), preferred_element_type=F32)


def dot_nn(a, b):
    return jnp.dot(a, b, preferred_element_type=F32)


def split3(v):
    hi = v.astype(BF16)
    rest = v - hi.astype(F32)
    mid = rest.astype(BF16)
    lo = (rest - mid.astype(F32)).astype(BF16)
    return hi, mid, lo


def pair_fwd_kernel(x_ref, w_ref, bias_ref, inv_ref, mean_ref):
    rows, keys, chan = x_ref.shape
    heads = bias_ref.shape[0]
    w = w_ref[...]
    ones = jnp.full((8, chan), 1.0, BF16)
    for base in range(0, rows, 8):
        parts = []
        invs = []
        means = []
        for i in range(base, base + 8):
            x = x_ref[i]
            raw = dot_nt(w, x)
            mean = raw[3 * heads : 3 * heads + 1] * (1.0 / chan)
            wide = x.astype(F32)
            centred = wide - jnp.mean(wide, axis=-1, keepdims=True)
            square = (centred * centred).astype(BF16)
            var = dot_nt(ones, square)[0:1] * (1.0 / chan)
            inv = lax.rsqrt(var + EPS)
            parts.append((raw[:heads] + raw[heads : 2 * heads] + raw[2 * heads : 3 * heads]) * inv)
            invs.append(inv)
            means.append(mean)
        block = jnp.stack(parts, axis=0)
        bias_ref[:, base : base + 8, :] = pltpu.einshape("ihj->hij", block).astype(BF16)
        inv_ref[base : base + 8, :] = jnp.concatenate(invs, axis=0)
        mean_ref[base : base + 8, :] = jnp.concatenate(means, axis=0)


def pair_fwd(x, w, heads, tile=32):
    rows, keys, chan = x.shape
    return pl.pallas_call(
        pair_fwd_kernel,
        grid=(rows // tile,),
        in_specs=[
            pl.BlockSpec((tile, keys, chan), lambda i: (i, 0, 0)),
            pl.BlockSpec(w.shape, lambda i: (0, 0)),
        ],
        out_specs=[
            pl.BlockSpec((heads, tile, keys), lambda i: (0, i, 0)),
            pl.BlockSpec((tile, keys), lambda i: (i, 0)),
            pl.BlockSpec((tile, keys), lambda i: (i, 0)),
        ],
        out_shape=[
            jax.ShapeDtypeStruct((heads, rows, keys), BF16),
            jax.ShapeDtypeStruct((rows, keys), F32),
            jax.ShapeDtypeStruct((rows, keys), F32),
        ],
        cost_estimate=pl.CostEstimate(flops=0, transcendentals=0, bytes_accessed=96 << 20),
        name="pair_fwd",
    )(x, w)


def attn_kernel(
    half_ref, q_ref, ko_ref, vo_ref, kr_ref, vr_ref, ga_ref, bias_ref, inv_ref, mean_ref, segc_ref, segr_ref, padr_ref,
    att_ref, dq_ref, own_ref, send_ref, r_ref, t_ref, s_ref,
    k_sc, v_sc, mask_sc, dk_sc, dv_sc, m2_sc,
):
    rows = q_ref.shape[0]
    heads, _, keys = bias_ref.shape
    size = q_ref.shape[1] // heads
    scale = 1.0 / math.sqrt(size)
    half = half_ref[0]
    own = pl.ds(pl.multiple_of(half * rows, 32), rows)
    other = pl.ds(pl.multiple_of((1 - half) * rows, 32), rows)
    k_sc[own, :] = ko_ref[...]
    k_sc[other, :] = kr_ref[...]
    v_sc[own, :] = vo_ref[...]
    v_sc[other, :] = vr_ref[...]

    @pl.when(pl.program_id(0) == 0)
    def _():
        row_id = lax.broadcasted_iota(jnp.int32, (rows, keys), 0) + half * rows
        col_id = lax.broadcasted_iota(jnp.int32, (rows, keys), 1)
        allowed = (segc_ref[...] == segr_ref[...]) & ((padr_ref[...] == 1) | (row_id == col_id))
        mask_sc[...] = jnp.where(allowed, 0.0, NEG)
        m2_sc[...] = jnp.zeros_like(m2_sc)

    inv = inv_ref[...]
    m2 = m2_sc[...]
    for h in range(heads):
        cut = slice(h * size, (h + 1) * size)
        qh = q_ref[:, cut]
        kh = k_sc[:, cut]
        vh = v_sc[:, cut]
        gh = ga_ref[:, cut]
        bias = bias_ref[h].astype(F32)
        scores = dot_nt(qh, kh) * scale + bias + mask_sc[...]
        top = jnp.max(scores, axis=-1, keepdims=True)
        e = jnp.exp(scores - top)
        p = e * (1.0 / jnp.sum(e, axis=-1, keepdims=True))
        low = p.astype(BF16)
        att_ref[:, cut] = dot_nn(low, vh).astype(BF16)
        gp = dot_nt(gh, vh)
        pg = p * gp
        delta = jnp.sum(pg, axis=-1, keepdims=True)
        gs32 = pg - p * delta
        gs = gs32.astype(BF16)
        dq_ref[:, cut] = (dot_nn(gs, kh) * scale).astype(BF16)
        dk_sc[:, cut] = dot_tn(gs, qh) * scale
        dv_sc[:, cut] = dot_tn(low, gh)
        m2 = m2 + gs32 * bias
        r_ref[h] = (gs.astype(F32) * inv).astype(BF16)
    m2_sc[...] = m2
    own_ref[0] = dk_sc[own, :]
    own_ref[1] = dv_sc[own, :]
    send_ref[0] = dk_sc[other, :]
    send_ref[1] = dv_sc[other, :]

    @pl.when(pl.program_id(0) == pl.num_programs(0) - 1)
    def _():
        slope = inv * inv * m2 * (1.0 / 128.0)
        s_ref[...] = -slope
        t_ref[...] = slope * mean_ref[...]


def attention(half, q, kv, kv_other, ga, bias, inv, mean, segc, segr, padr):
    rows, width = q.shape
    heads, _, keys = bias.shape
    groups = 2
    part = width // groups

    def lanes(first):
        return pl.BlockSpec((rows, part), lambda g: (0, first + g))

    def fixed(shape):
        return pl.BlockSpec(shape, lambda g: (0,) * len(shape))

    plane = fixed((rows, keys))
    pair = pl.BlockSpec((2, rows, part), lambda g: (0, 0, g))
    head = pl.BlockSpec((heads // groups, rows, keys), lambda g: (g, 0, 0))
    return pl.pallas_call(
        attn_kernel,
        grid=(groups,),
        in_specs=[
            pl.BlockSpec(memory_space=pltpu.SMEM),
            lanes(0), lanes(0), lanes(groups), lanes(0), lanes(groups), lanes(0), head, plane, plane,
            fixed(segc.shape), fixed(segr.shape), fixed(padr.shape),
        ],
        out_specs=[lanes(0), lanes(0), pair, pair, head, plane, plane],
        out_shape=[
            jax.ShapeDtypeStruct((rows, width), BF16),
            jax.ShapeDtypeStruct((rows, width), BF16),
            jax.ShapeDtypeStruct((2, rows, width), F32),
            jax.ShapeDtypeStruct((2, rows, width), F32),
            jax.ShapeDtypeStruct((heads, rows, keys), BF16),
            jax.ShapeDtypeStruct((rows, keys), F32),
            jax.ShapeDtypeStruct((rows, keys), F32),
        ],
        scratch_shapes=[
            pltpu.VMEM((keys, part), BF16),
            pltpu.VMEM((keys, part), BF16),
            pltpu.VMEM((rows, keys), F32),
            pltpu.VMEM((keys, part), F32),
            pltpu.VMEM((keys, part), F32),
            pltpu.VMEM((rows, keys), F32),
        ],
        cost_estimate=pl.CostEstimate(flops=0, transcendentals=0, bytes_accessed=60 << 20),
        name="attn",
    )(half, q, kv, kv, kv_other, kv_other, ga, bias, inv, mean, segc, segr, padr)


def pair_bwd_kernel(x_ref, r_ref, t_ref, s_ref, mean_ref, w_ref, out_ref, n_ref, c_ref):
    rows, keys, chan = x_ref.shape
    heads = r_ref.shape[0]
    depth = w_ref.shape[0]
    w = w_ref[...]

    @pl.when(pl.program_id(0) == 0)
    def _():
        n_ref[...] = jnp.zeros_like(n_ref)
        c_ref[...] = jnp.zeros_like(c_ref)

    acc = jnp.zeros(n_ref.shape, F32)
    corr = jnp.zeros(c_ref.shape, F32)
    pad = jnp.zeros((depth - 2 * heads - 6, keys), F32)
    for base in range(0, rows, 8):
        block = pltpu.einshape("hij->ihj", r_ref[:, base : base + 8, :].astype(F32))
        for k in range(8):
            i = base + k
            r32 = block[k]
            t = t_ref[i : i + 1, :]
            s = s_ref[i : i + 1, :]
            th, tm, tl = (v.astype(F32) for v in split3(t))
            sh, sm, sl = (v.astype(F32) for v in split3(s))
            left = jnp.concatenate([r32, r32, th, tm, tl, sh, sm, sl, pad], axis=0).astype(BF16)
            both = dot_tn(left, w)
            x = x_ref[i]
            out_ref[i] = (both[:, :chan] + x.astype(F32) * both[:, chan:]).astype(BF16)
            acc = acc + dot_nn(r32.astype(BF16), x)
            corr = corr + r32 * mean_ref[i : i + 1, :]
    n_ref[...] += acc
    c_ref[...] += corr


def pair_bwd(x, r, t, s, mean, w, tile=32):
    rows, keys, chan = x.shape
    heads = r.shape[0]
    return pl.pallas_call(
        pair_bwd_kernel,
        grid=(rows // tile,),
        in_specs=[
            pl.BlockSpec((tile, keys, chan), lambda i: (i, 0, 0)),
            pl.BlockSpec((heads, tile, keys), lambda i: (0, i, 0)),
            pl.BlockSpec((tile, keys), lambda i: (i, 0)),
            pl.BlockSpec((tile, keys), lambda i: (i, 0)),
            pl.BlockSpec((tile, keys), lambda i: (i, 0)),
            pl.BlockSpec(w.shape, lambda i: (0, 0)),
        ],
        out_specs=[
            pl.BlockSpec((tile, keys, chan), lambda i: (i, 0, 0)),
            pl.BlockSpec((heads, chan), lambda i: (0, 0)),
            pl.BlockSpec((heads, keys), lambda i: (0, 0)),
        ],
        out_shape=[
            jax.ShapeDtypeStruct((rows, keys, chan), BF16),
            jax.ShapeDtypeStruct((heads, chan), F32),
            jax.ShapeDtypeStruct((heads, keys), F32),
        ],
        cost_estimate=pl.CostEstimate(flops=0, transcendentals=0, bytes_accessed=60 << 20),
        name="pair_bwd",
    )(x, r, t, s, mean, w)


def norm_rows(values):
    centred = values - jnp.mean(values, -1, keepdims=True)
    inverse = lax.rsqrt(jnp.mean(centred * centred, -1, keepdims=True) + EPS)
    return (centred * inverse, inverse)


def norm_back(incoming, normal, inverse):
    return inverse * (
        incoming
        - jnp.mean(incoming, -1, keepdims=True)
        - normal * jnp.mean(incoming * normal, -1, keepdims=True)
    )


def sigmoid(v):
    return jax.nn.sigmoid(v)


def fetch(pairs, sems):
    copies = [pltpu.make_async_copy(src, dst, sems.at[k]) for k, (src, dst) in enumerate(pairs)]
    for copy in copies:
        copy.start()
    return copies


def put(side, own_ref, send_ref, start, low, high):
    stop = start + low.shape[1]

    @pl.when(side == 0)
    def _():
        own_ref[:, start:stop] = low
        send_ref[:, start:stop] = high

    @pl.when(side != 0)
    def _():
        own_ref[:, start:stop] = high
        send_ref[:, start:stop] = low


def total(v):
    return jnp.sum(v.astype(F32), axis=0, keepdims=True)


def pair_weights(gain_ref, weight_ref, forward_ref, backward_ref):
    gained = weight_ref[...].astype(F32) * gain_ref[...].astype(F32)
    heads, chan = gained.shape
    hi, mid, lo = split3(gained - jnp.mean(gained, axis=1, keepdims=True))
    forward_ref[0:heads, :] = hi
    forward_ref[heads : 2 * heads, :] = mid
    forward_ref[2 * heads : 3 * heads, :] = lo
    row = lax.broadcasted_iota(jnp.int32, (16, chan), 0)
    forward_ref[3 * heads :, :] = jnp.where(row == 0, 1.0, 0.0).astype(BF16)
    backward_ref[0:heads, :chan] = hi
    backward_ref[heads : 2 * heads, :chan] = mid
    backward_ref[0 : 2 * heads, chan:] = jnp.zeros((2 * heads, chan), BF16)
    backward_ref[2 * heads :, :chan] = jnp.where(row < 3, 1.0, 0.0).astype(BF16)
    backward_ref[2 * heads :, chan:] = jnp.where((row >= 3) & (row < 6), 1.0, 0.0).astype(BF16)


def trans_kernel(
    side_ref, single_ref, cond_ref, cot_ref, gain_ref, bias_ref, pair_gain_ref, pair_weight_ref, cw_hbm, ew_hbm, tw_hbm,
    x_hbm, scale0_hbm, keep0_hbm,
    own_ref, send_ref, kept_ref, grad_norm_ref, grad_cond_ref, grad_direct_ref, sums_ref, gain_sum_ref,
    forward_ref, backward_ref,
    cw, ew, tw, x_ref, scale0_ref, keep0_ref, scale1_ref, sems, out_sems,
):
    order = (3, 4, 5, 0, 1, 2)
    copies = fetch(
        [(cw_hbm.at[k], cw.at[k]) for k in order[:3]]
        + [(ew_hbm.at[0], ew.at[0]), (ew_hbm.at[1], ew.at[1]), (tw_hbm, tw)]
        + [(cw_hbm.at[k], cw.at[k]) for k in order[3:]],
        sems,
    )
    side = side_ref[0]
    rows, width = single_ref.shape
    cond_width = cond_ref.shape[1]
    cut = width // 2
    hidden_width = tw.shape[0]
    pair_weights(pair_gain_ref, pair_weight_ref, forward_ref, backward_ref)
    single_norm, _ = norm_rows(single_ref[...].astype(F32))
    cond_norm, _ = norm_rows(cond_ref[...].astype(F32))
    cond = cond_ref[...]
    x_ref[:, 2 * width + 2 * cond_width :] = cond

    def modulate(b, waits, scale_ref):
        low = (cond_norm * gain_ref[b : b + 1, :].astype(F32)).astype(BF16)
        x_ref[:, 2 * width + b * cond_width : 2 * width + (b + 1) * cond_width] = low
        waits[0].wait()
        scale = sigmoid(dot_nn(low, cw[3 * b]) + bias_ref[2 * b : 2 * b + 1, :].astype(F32))
        scale_ref[...] = scale
        waits[1].wait()
        shift = dot_nn(low, cw[3 * b + 1])
        x_ref[:, b * width : (b + 1) * width] = (scale * single_norm + shift).astype(BF16)
        waits[2].wait()
        return sigmoid(dot_nn(cond, cw[3 * b + 2]) + bias_ref[2 * b + 1 : 2 * b + 2, :].astype(F32))

    keep = modulate(1, copies[:3], scale1_ref)
    keep0_ref[...] = modulate(0, copies[6:], scale0_ref)
    leaving = fetch([(x_ref, x_hbm), (scale0_ref, scale0_hbm), (keep0_ref, keep0_hbm)], out_sems)
    trans_in = x_ref[:, width : 2 * width]
    upstream = cot_ref[...].astype(F32)
    grad_trans = (upstream * keep).astype(BF16)
    at = hidden_width
    put(side, own_ref, send_ref, at + hidden_width, grad_trans[:, :cut], grad_trans[:, cut:])
    for copy in copies[3:6]:
        copy.wait()
    grad_in = jnp.zeros((rows, width), F32)
    trans_out = jnp.zeros((rows, width), F32)
    step = 512
    for c in range(0, hidden_width, step):
        span = slice(c, c + step)
        gate_pre = dot_nn(trans_in, ew[0, :, span])
        up_pre = dot_nn(trans_in, ew[1, :, span])
        sig = sigmoid(gate_pre)
        act = gate_pre * sig
        hidden = (act * up_pre).astype(BF16)
        own_ref[:, span] = hidden
        send_ref[:, span] = hidden
        trans_out = trans_out + dot_nn(hidden, tw[span, :])
        grad_hidden = dot_nt(grad_trans, tw[span, :])
        grad_gate = (grad_hidden * up_pre * sig * (1.0 + gate_pre * (1.0 - sig))).astype(BF16)
        grad_up = (grad_hidden * act).astype(BF16)
        put(side, own_ref, send_ref, at + c, grad_gate, grad_up)
        grad_in = grad_in + dot_nt(grad_gate, ew[0, :, span]) + dot_nt(grad_up, ew[1, :, span])
    kept_ref[...] = keep * trans_out
    grad_keep = (upstream * trans_out * keep * (1.0 - keep)).astype(BF16)
    finish_branch(
        side, 1, 2 * hidden_width + cut, (), cw.at[3:6], single_ref, cond_ref, gain_ref, scale1_ref, grad_in, grad_keep,
        own_ref, send_ref, grad_norm_ref, grad_cond_ref, grad_direct_ref, sums_ref, gain_sum_ref,
    )
    for copy in leaving:
        copy.wait()


def trans(side, single, cond, cot, gains, biases, pair_gain, pair_weight, cw, ew, tw):
    rows, width = single.shape
    cond_width = cond.shape[1]
    hidden_width = tw.shape[0]
    heads, chan = pair_weight.shape
    packed = 2 * hidden_width + width // 2 + width + width // 2
    x_width = 2 * width + 3 * cond_width
    vm = pl.BlockSpec(memory_space=pltpu.VMEM)
    hbm = pl.BlockSpec(memory_space=pl.ANY)
    wide = jax.ShapeDtypeStruct((rows, width), F32)
    narrow = jax.ShapeDtypeStruct((rows, cond_width), F32)
    return pl.pallas_call(
        trans_kernel,
        in_specs=[pl.BlockSpec(memory_space=pltpu.SMEM)] + [vm] * 7 + [hbm] * 3,
        out_specs=[hbm] * 3 + [vm] * 10,
        out_shape=[
            jax.ShapeDtypeStruct((rows, x_width), BF16),
            wide,
            wide,
            jax.ShapeDtypeStruct((rows, packed), BF16),
            jax.ShapeDtypeStruct((rows, packed), BF16),
            wide,
            wide,
            narrow,
            narrow,
            jax.ShapeDtypeStruct((2, width), F32),
            jax.ShapeDtypeStruct((1, cond_width), F32),
            jax.ShapeDtypeStruct((3 * heads + 16, chan), BF16),
            jax.ShapeDtypeStruct((2 * heads + 16, 2 * chan), BF16),
        ],
        scratch_shapes=[
            pltpu.VMEM(cw.shape, BF16),
            pltpu.VMEM(ew.shape, BF16),
            pltpu.VMEM(tw.shape, BF16),
            pltpu.VMEM((rows, x_width), BF16),
            pltpu.VMEM((rows, width), F32),
            pltpu.VMEM((rows, width), F32),
            pltpu.VMEM((rows, width), F32),
            pltpu.SemaphoreType.DMA((9,)),
            pltpu.SemaphoreType.DMA((3,)),
        ],
        cost_estimate=pl.CostEstimate(flops=0, transcendentals=0, bytes_accessed=50 << 20),
        name="trans",
    )(side, single, cond, cot, gains, biases, pair_gain, pair_weight, cw, ew, tw)


def finish_branch(
    side, b, at, copies, cw, single_ref, cond_ref, gain_ref, scale_ref, grad_in, grad_keep,
    own_ref, send_ref, grad_norm_ref, grad_cond_ref, grad_direct_ref, sums_ref, gain_sum_ref,
):
    width = single_ref.shape[1]
    cut = width // 2
    single_norm, _ = norm_rows(single_ref[...].astype(F32))
    cond_norm, _ = norm_rows(cond_ref[...].astype(F32))
    scale = scale_ref[...]
    grad_scale = (grad_in * single_norm * scale * (1.0 - scale)).astype(BF16)
    grad_shift = grad_in.astype(BF16)
    put(side, own_ref, send_ref, at, grad_scale, grad_shift)
    put(side, own_ref, send_ref, at + width, grad_keep[:, :cut], grad_keep[:, cut:])
    grad_norm_ref[...] = grad_in * scale
    for copy in copies:
        copy.wait()
    grad_low = dot_nt(grad_scale, cw[0]) + dot_nt(grad_shift, cw[1])
    grad_cond_ref[...] = grad_low * gain_ref[b : b + 1, :].astype(F32)
    grad_direct_ref[...] = dot_nt(grad_keep, cw[2])
    gain_sum_ref[...] = total(grad_low * cond_norm)
    sums_ref[0:1, :] = total(grad_scale)
    sums_ref[1:2, :] = total(grad_keep)


def project_kernel(
    x_hbm, cot_ref, bias_ref, keep_hbm, aw_hbm, ow_hbm, q_ref, kv_ref, gate_ref, mixed_ref, attended_ref,
    x, keep, aw, ow, sems,
):
    width = cot_ref.shape[1]
    copies = fetch(
        [(x_hbm.at[:, :width], x)] + [(aw_hbm.at[k], aw.at[k]) for k in range(4)] + [(keep_hbm, keep), (ow_hbm, ow)], sems
    )
    copies[0].wait()
    copies[1].wait()
    q_ref[...] = (dot_nn(x[...], aw[0]) + bias_ref[4:5, :].astype(F32)).astype(BF16)
    copies[2].wait()
    kv_ref[:, :width] = dot_nn(x[...], aw[1]).astype(BF16)
    copies[3].wait()
    kv_ref[:, width:] = dot_nn(x[...], aw[2]).astype(BF16)
    copies[4].wait()
    gate = sigmoid(dot_nn(x[...], aw[3]))
    gate_ref[...] = gate
    copies[5].wait()
    grad_attn = (cot_ref[...].astype(F32) * keep[...]).astype(BF16)
    copies[6].wait()
    grad_mixed = dot_nt(grad_attn, ow[...])
    mixed_ref[...] = grad_mixed
    attended_ref[...] = (grad_mixed * gate).astype(BF16)


def project(x, cot, biases, keep, aw, ow):
    rows, width = cot.shape
    vm = pl.BlockSpec(memory_space=pltpu.VMEM)
    hbm = pl.BlockSpec(memory_space=pl.ANY)
    return pl.pallas_call(
        project_kernel,
        in_specs=[hbm, vm, vm, hbm, hbm, hbm],
        out_specs=[vm] * 5,
        out_shape=[
            jax.ShapeDtypeStruct((rows, width), BF16),
            jax.ShapeDtypeStruct((rows, 2 * width), BF16),
            jax.ShapeDtypeStruct((rows, width), F32),
            jax.ShapeDtypeStruct((rows, width), F32),
            jax.ShapeDtypeStruct((rows, width), BF16),
        ],
        scratch_shapes=[
            pltpu.VMEM((rows, width), BF16),
            pltpu.VMEM((rows, width), F32),
            pltpu.VMEM(aw.shape, BF16),
            pltpu.VMEM(ow.shape, BF16),
            pltpu.SemaphoreType.DMA((7,)),
        ],
        cost_estimate=pl.CostEstimate(flops=0, transcendentals=0, bytes_accessed=22 << 20),
        name="project",
    )(x, cot, biases, keep, aw, ow)


def after_kernel(
    side_ref, single_ref, cond_ref, cot_ref, gain_ref,
    attended_hbm, gate_hbm, ow_hbm, keep_hbm, kept_hbm, grad_q_hbm, dkv_own_hbm, dkv_recv_hbm, grad_mixed_hbm, aw_hbm,
    scale_hbm, cw_hbm, grad_norm1_hbm, grad_cond1_hbm, direct1_hbm,
    own_ref, send_ref, layer_hbm, grad_single_ref, grad_cond_ref, sums_ref, gain_sum_ref,
    attended_ref, gate_ref, ow, keep_ref, kept_ref, grad_q_ref, dkv_own_ref, dkv_recv_ref, grad_mixed_ref, aw,
    scale_ref, cw, grad_norm1_ref, grad_cond1_ref, direct1_ref, layer_ref, norm_sc, cond_sc, direct_sc, sems, out_sem,
):
    sources = [
        (attended_hbm, attended_ref), (gate_hbm, gate_ref), (ow_hbm, ow), (keep_hbm, keep_ref), (kept_hbm, kept_ref),
        (grad_q_hbm, grad_q_ref), (dkv_own_hbm, dkv_own_ref), (dkv_recv_hbm, dkv_recv_ref),
        (grad_mixed_hbm, grad_mixed_ref),
    ]
    sources += [(aw_hbm.at[k], aw.at[k]) for k in range(4)]
    sources += [(scale_hbm, scale_ref)] + [(cw_hbm.at[k], cw.at[k]) for k in range(3)]
    sources += [(grad_norm1_hbm, grad_norm1_ref), (grad_cond1_hbm, grad_cond1_ref), (direct1_hbm, direct1_ref)]
    copies = fetch(sources, sems)
    side = side_ref[0]
    width = single_ref.shape[1]
    cut = width // 2
    upstream = cot_ref[...].astype(F32)
    single_norm, single_inverse = norm_rows(single_ref[...].astype(F32))
    cond_norm, cond_inverse = norm_rows(cond_ref[...].astype(F32))
    copies[0].wait()
    copies[1].wait()
    gate = gate_ref[...]
    attended = attended_ref[...].astype(F32)
    mixed = (attended * gate).astype(BF16)
    own_ref[:, :width] = mixed
    send_ref[:, :width] = mixed
    copies[2].wait()
    attn_out = dot_nn(mixed, ow[...])
    copies[3].wait()
    keep = keep_ref[...]
    copies[4].wait()
    layer_ref[...] = (single_ref[...].astype(F32) + keep * attn_out + kept_ref[...]).astype(BF16)
    leaving = pltpu.make_async_copy(layer_ref, layer_hbm, out_sem)
    leaving.start()
    grad_keep = (upstream * attn_out * keep * (1.0 - keep)).astype(BF16)
    grad_attn = (upstream * keep).astype(BF16)
    put(side, own_ref, send_ref, 3 * width, grad_attn[:, :cut], grad_attn[:, cut:])
    for copy in copies[5:9]:
        copy.wait()
    grad_q = grad_q_ref[...]
    grad_k = (dkv_own_ref[0] + dkv_recv_ref[0]).astype(BF16)
    grad_v = (dkv_own_ref[1] + dkv_recv_ref[1]).astype(BF16)
    grad_logit = (grad_mixed_ref[...] * attended * gate * (1.0 - gate)).astype(BF16)
    put(side, own_ref, send_ref, width, grad_q, grad_v)
    put(side, own_ref, send_ref, 2 * width, grad_k, grad_logit)
    sums_ref[2:3, :] = total(grad_q)
    grad_in = jnp.zeros(single_ref.shape, F32)
    for k, part in enumerate((grad_q, grad_k, grad_v, grad_logit)):
        copies[9 + k].wait()
        grad_in = grad_in + dot_nt(part, aw[k])
    copies[13].wait()
    finish_branch(
        side, 0, 3 * width + cut, copies[14:17], cw, single_ref, cond_ref, gain_ref, scale_ref, grad_in, grad_keep,
        own_ref, send_ref, norm_sc, cond_sc, direct_sc, sums_ref, gain_sum_ref,
    )
    for copy in copies[17:]:
        copy.wait()
    grad_single_ref[...] = upstream + norm_back(norm_sc[...] + grad_norm1_ref[...], single_norm, single_inverse)
    grad_cond_ref[...] = (
        norm_back(cond_sc[...] + grad_cond1_ref[...], cond_norm, cond_inverse) + (direct_sc[...] + direct1_ref[...])
    )
    leaving.wait()


def after(side, single, cond, cot, gains, attended, gate, ow, keep, kept, grad_q, dkv_own, dkv_recv, grad_mixed, aw,
          scale, cw, grad_norm1, grad_cond1, direct1):
    rows, width = single.shape
    cond_width = cond.shape[1]
    packed = 3 * width + width // 2 + width + width // 2
    vm = pl.BlockSpec(memory_space=pltpu.VMEM)
    hbm = pl.BlockSpec(memory_space=pl.ANY)
    moved = (attended, gate, ow, keep, kept, grad_q, dkv_own, dkv_recv, grad_mixed, aw, scale, cw,
             grad_norm1, grad_cond1, direct1)
    shapes = [(3,) + v.shape[1:] if v is cw else v.shape for v in moved]
    return pl.pallas_call(
        after_kernel,
        in_specs=[pl.BlockSpec(memory_space=pltpu.SMEM)] + [vm] * 4 + [hbm] * len(moved),
        out_specs=[vm, vm, hbm] + [vm] * 4,
        out_shape=[
            jax.ShapeDtypeStruct((rows, packed), BF16),
            jax.ShapeDtypeStruct((rows, packed), BF16),
            jax.ShapeDtypeStruct((rows, width), BF16),
            jax.ShapeDtypeStruct((rows, width), F32),
            jax.ShapeDtypeStruct((rows, cond_width), F32),
            jax.ShapeDtypeStruct((3, width), F32),
            jax.ShapeDtypeStruct((1, cond_width), F32),
        ],
        scratch_shapes=[pltpu.VMEM(shape, v.dtype) for shape, v in zip(shapes, moved)]
        + [
            pltpu.VMEM((rows, width), BF16),
            pltpu.VMEM((rows, width), F32),
            pltpu.VMEM((rows, cond_width), F32),
            pltpu.VMEM((rows, cond_width), F32),
            pltpu.SemaphoreType.DMA((20,)),
            pltpu.SemaphoreType.DMA,
        ],
        cost_estimate=pl.CostEstimate(flops=0, transcendentals=0, bytes_accessed=40 << 20),
        name="after",
    )(side, single, cond, cot, gains, *moved)


TILE = 384


def place(position, order):
    count = len(order)
    return sum(((position >> (count - 1 - j)) & 1) << order[j] for j in range(count))


def wgrad_kernel(plan, orders, me_ref, *refs):
    sources, outs = refs[:4], refs[4:8]
    (x_own, x_recv, g_own, g_recv), turned_ref, results, sems, out_sems = refs[8:12], refs[12], refs[13:17], refs[17], refs[18]
    copies = fetch(list(zip(sources, (x_own, x_recv, g_own, g_recv))), sems)
    copies[0].wait()
    copies[1].wait()
    me = me_ref[0]
    blocks = 1 << len(orders[0])
    last = [max(k for k, group in enumerate(plan) if any(use[1] == color for use in group[3])) for color in (0, 1)]
    leaving = []
    for k, (source, start, width, uses) in enumerate(plan):
        height = width // blocks
        own, recv = ((x_own, x_recv), (g_own, g_recv))[source]
        span = slice(start, start + width)
        turned_ref[:width, :] = jnp.concatenate([own[:, span], recv[:, span]], axis=0).astype(F32).T
        if k == 0:
            copies[2].wait()
            copies[3].wait()
        for color in (0, 1):
            mine = [use for use in uses if use[1] == color]
            if mine:
                left = jnp.concatenate(
                    [
                        turned_ref[pl.ds(pl.multiple_of((me ^ place(p, orders[color])) * height, 8), height), :]
                        for p in range(blocks)
                    ],
                    axis=0,
                ).astype(BF16)
            keep_ref, send_ref = results[2 * color], results[2 * color + 1]
            for column, _, offset in mine:
                cut = slice(column, column + TILE)
                term = dot_nn(left, jnp.concatenate([g_own[:, cut], g_recv[:, cut]], axis=0)).astype(BF16)
                for p in range(blocks):
                    target = keep_ref if p < blocks // 2 else send_ref
                    target[p % (blocks // 2), offset : offset + height, :] = term[p * height : (p + 1) * height]
            if k == last[color]:
                for j in (2 * color, 2 * color + 1):
                    copy = pltpu.make_async_copy(results[j], outs[j], out_sems.at[j])
                    copy.start()
                    leaving.append(copy)
    for copy in leaving:
        copy.wait()


def wgrad(me, x_own, x_recv, g_own, g_recv, plan, orders, totals, name):
    rows = x_own.shape[0]
    blocks = 1 << len(orders[0])
    half = blocks // 2
    if any((width // blocks) % 8 for _, _, width, _ in plan):
        return wgrad_plain(me, x_own, x_recv, g_own, g_recv, plan, orders, totals)
    hbm = pl.BlockSpec(memory_space=pl.ANY)
    shapes = [(half, count, TILE) for count in totals for _ in range(2)]
    widest = max(group[2] for group in plan)
    moved = (x_own, x_recv, g_own, g_recv)
    return pl.pallas_call(
        functools.partial(wgrad_kernel, plan, orders),
        in_specs=[pl.BlockSpec(memory_space=pltpu.SMEM)] + [hbm] * 4,
        out_specs=[hbm] * 4,
        out_shape=[jax.ShapeDtypeStruct(shape, BF16) for shape in shapes],
        scratch_shapes=[pltpu.VMEM(v.shape, v.dtype) for v in moved]
        + [pltpu.VMEM((widest, 2 * rows), F32)]
        + [pltpu.VMEM(shape, BF16) for shape in shapes]
        + [pltpu.SemaphoreType.DMA((4,)), pltpu.SemaphoreType.DMA((4,))],
        cost_estimate=pl.CostEstimate(flops=0, transcendentals=0, bytes_accessed=26 << 20),
        name=name,
    )(me, *moved)


def wgrad_plain(me, x_own, x_recv, g_own, g_recv, plan, orders, totals):
    blocks = 1 << len(orders[0])
    pieces = ([], [])
    for source, start, width, uses in plan:
        own, recv = ((x_own, x_recv), (g_own, g_recv))[source]
        x = jnp.concatenate([own[:, start : start + width], recv[:, start : start + width]], axis=0)
        for column, color, offset in uses:
            g = jnp.concatenate([g_own[:, column : column + TILE], g_recv[:, column : column + TILE]], axis=0)
            wanted = jnp.stack([me[0] ^ place(p, orders[color]) for p in range(blocks)])
            term = jnp.take(dot_tn(x, g).reshape(blocks, width // blocks, TILE), wanted, axis=0)
            pieces[color].append((offset, term.astype(BF16)))
    outs = []
    for parts in pieces:
        whole = jnp.concatenate([term for _, term in sorted(parts, key=lambda part: part[0])], axis=1)
        outs += [whole[: blocks // 2], whole[blocks // 2 :]]
    return outs


def send_half(value, bit):
    count = lax.axis_size("crop")
    return lax.ppermute(value, "crop", [(i, i ^ (1 << bit)) for i in range(count)])


def arrivals(state, j, orders):
    return [send_half(send, order[j]) for (_, send), order in zip(state, orders)]


def add_kernel(*refs):
    if refs[0].shape[0] == 1 and len(refs) == 6:
        for color in (0, 1):
            refs[4 + color][...] = refs[2 * color][0].astype(F32) + refs[2 * color + 1][0].astype(F32)
        return
    for color in (0, 1):
        low, high, other_low, other_high = refs[4 * color : 4 * color + 4]
        keep, send = refs[8 + 2 * color : 10 + 2 * color]
        keep[...] = (low[...].astype(F32) + other_low[...].astype(F32)).astype(BF16)
        send[...] = (high[...].astype(F32) + other_high[...].astype(F32)).astype(BF16)


def added(state, arrived, name):
    count = state[0][0].shape[0]
    half = count // 2
    operands, in_specs, out_specs, out_shape = [], [], [], []
    for (keep, _), other in zip(state, arrived):
        block = (1,) + keep.shape[1:]
        if half:
            low = pl.BlockSpec(block, lambda p: (p, 0, 0))
            high = pl.BlockSpec(block, lambda p: (p + half, 0, 0))
            operands += [keep, keep, other, other]
            in_specs += [low, high, low, high]
            out_specs += [low, low]
            out_shape += [jax.ShapeDtypeStruct((half,) + keep.shape[1:], BF16)] * 2
        else:
            operands += [keep, other]
            in_specs += [pl.BlockSpec(memory_space=pltpu.VMEM)] * 2
            out_specs += [pl.BlockSpec(memory_space=pltpu.VMEM)]
            out_shape += [jax.ShapeDtypeStruct(keep.shape[1:], F32)]
    out = pl.pallas_call(
        add_kernel,
        grid=(half,) if half else (),
        in_specs=in_specs,
        out_specs=out_specs,
        out_shape=out_shape,
        cost_estimate=pl.CostEstimate(flops=0, transcendentals=0, bytes_accessed=2 << 20),
        name=name,
    )(*operands)
    return [(out[0], out[1]), (out[2], out[3])] if half else [(v, None) for v in out]


def swap(v):
    return lax.ppermute(v, "seq", [(0, 1), (1, 0)])


def rows_of(side, ref, offset, height):
    v = ref[offset : offset + height, :]
    return jnp.where(side == 0, v[: height // 2], v[height // 2 :])


def sides(side, mine_ref, recv_ref, offset, height):
    mine = rows_of(side, mine_ref, offset, height)
    recv = rows_of(side, recv_ref, offset, height)
    return jnp.where(side == 0, mine, recv), jnp.where(side == 0, recv, mine)


def close_trans_kernel(tall, long, flat, side_ref, a_ref, b_ref, ra_ref, rb_ref, expand_ref, contract_ref, cond_ref):
    side = side_ref[0]
    for t in range(4):
        refs = (a_ref, ra_ref, t * tall) if t < 3 else (b_ref, rb_ref, 0)
        low, high = sides(side, *refs, tall)
        expand_ref[:, 0, t * TILE : (t + 1) * TILE] = low
        expand_ref[:, 1, t * TILE : (t + 1) * TILE] = high
    low, high = sides(side, b_ref, rb_ref, tall, long)
    contract_ref[:, :TILE] = low
    contract_ref[:, TILE:] = high
    low, high = sides(side, a_ref, ra_ref, 3 * tall, flat)
    cond_ref[0, :, :TILE] = low
    cond_ref[1, :, :TILE] = high
    low, high = sides(side, b_ref, rb_ref, tall + long, flat)
    cond_ref[0, :, TILE:] = low
    cond_ref[1, :, TILE:] = high
    low, high = sides(side, b_ref, rb_ref, tall + long + flat, flat)
    cond_ref[2, :, :TILE] = low
    cond_ref[2, :, TILE:] = high


def close_attn_kernel(tall, flat, side_ref, a_ref, b_ref, ra_ref, rb_ref, cond_in, attn_ref, out_ref, cond_ref):
    side = side_ref[0]
    for t in range(4):
        refs = (a_ref, ra_ref, t * tall) if t < 3 else (b_ref, rb_ref, 0)
        low, high = sides(side, *refs, tall)
        cut = slice((t % 2) * TILE, (t % 2 + 1) * TILE)
        attn_ref[:, t // 2, cut] = low
        attn_ref[:, 2 + t // 2, cut] = high
    low, high = sides(side, b_ref, rb_ref, tall, tall)
    out_ref[:, :TILE] = low
    out_ref[:, TILE:] = high
    for t in range(2):
        low, high = sides(side, b_ref, rb_ref, 2 * tall + t * flat, flat)
        cond_ref[:, 0, t * TILE : (t + 1) * TILE] = low
        cond_ref[:, 1, t * TILE : (t + 1) * TILE] = high
    low, high = sides(side, b_ref, rb_ref, 2 * tall + 2 * flat, flat)
    cond_ref[:, 2, :TILE] = low
    cond_ref[:, 2, TILE:] = high
    for k in range(3):
        cond_ref[:, 3 + k, :] = cond_in[k]


def close(kernel, side, operands, shapes, name):
    vm = pl.BlockSpec(memory_space=pltpu.VMEM)
    return pl.pallas_call(
        kernel,
        in_specs=[pl.BlockSpec(memory_space=pltpu.SMEM)] + [vm] * len(operands),
        out_specs=[vm] * len(shapes),
        out_shape=[jax.ShapeDtypeStruct(shape, F32) for shape in shapes],
        cost_estimate=pl.CostEstimate(flops=0, transcendentals=0, bytes_accessed=4 << 20),
        name=name,
    )(side, *operands)


def small_kernel(
    groups, me_ref, sums0_ref, sums1_ref, gain0_ref, gain1_ref, n_ref, c_ref, pair_gain_ref, pair_weight_ref, *refs
):
    outs, tiles_ref = refs[:-1], refs[-1]
    devices = tiles_ref.shape[0]
    heads, chan = n_ref.shape
    normed = n_ref[...] - jnp.sum(c_ref[...], axis=1, keepdims=True)
    to_weight = (normed * pair_gain_ref[...].astype(F32)).T
    to_gain = total(pair_weight_ref[...].astype(F32) * normed)
    biases = jnp.concatenate([sums0_ref[0:2, :], sums1_ref[...], sums0_ref[2:3, :]], axis=0)
    gains = jnp.concatenate([gain0_ref[...], gain1_ref[...]], axis=0)
    wide, thin, part = biases.shape[1] // devices, gains.shape[1] // devices, chan // devices
    for d in range(devices):
        tiles_ref[d] = jnp.zeros(tiles_ref.shape[1:], F32)
        tiles_ref[d, 0:5, 0:wide] = biases[:, d * wide : (d + 1) * wide]
        tiles_ref[d, 0:2, 32 : 32 + thin] = gains[:, d * thin : (d + 1) * thin]
        tiles_ref[d, 0:1, 64 : 64 + part] = to_gain[:, d * part : (d + 1) * part]
        tiles_ref[d, 0:part, 96 : 96 + heads] = to_weight[d * part : (d + 1) * part, :]
    me = me_ref[0]
    step = len(outs)
    for m, out in enumerate(outs):
        for k in range(out.shape[0]):
            out[k] = tiles_ref[pl.ds(2 * (me ^ (k * step + m)), 2)]


def small_sums(me, crops, groups, *operands):
    step = 1 << groups[0]
    vm = pl.BlockSpec(memory_space=pltpu.VMEM)
    return pl.pallas_call(
        functools.partial(small_kernel, groups),
        in_specs=[pl.BlockSpec(memory_space=pltpu.SMEM)] + [vm] * len(operands),
        out_specs=[vm] * step,
        out_shape=[jax.ShapeDtypeStruct((crops // step, 2, 8, 128), F32)] * step,
        scratch_shapes=[pltpu.VMEM((2 * crops, 8, 128), F32)],
        cost_estimate=pl.CostEstimate(flops=0, transcendentals=0, bytes_accessed=4 << 20),
        name="small_sums",
    )(me, *operands)


def spread(parts, shift):
    count = lax.axis_size("crop")
    return [
        lax.ppermute(part, "crop", [(i, i ^ (m << shift)) for i in range(count)]) for m, part in enumerate(parts) if m
    ]


def flipped(index, mask):
    out, bit = index, 1
    while bit <= mask:
        if mask & bit:
            out = out + (1 - 2 * ((index // bit) % 2)) * bit
        bit *= 2
    return out


def small_tiles(tiles_ref, sums0_ref, sums1_ref, gain0_ref, gain1_ref, n_ref, c_ref, pair_gain_ref, pair_weight_ref):
    devices = tiles_ref.shape[0]
    heads, chan = n_ref.shape
    normed = n_ref[...] - jnp.sum(c_ref[...], axis=1, keepdims=True)
    to_weight = (normed * pair_gain_ref[...].astype(F32)).T
    to_gain = total(pair_weight_ref[...].astype(F32) * normed)
    biases = jnp.concatenate([sums0_ref[0:2, :], sums1_ref[...], sums0_ref[2:3, :]], axis=0)
    gains = jnp.concatenate([gain0_ref[...], gain1_ref[...]], axis=0)
    wide, thin, part = biases.shape[1] // devices, gains.shape[1] // devices, chan // devices
    for d in range(devices):
        tiles_ref[d] = jnp.zeros(tiles_ref.shape[1:], F32)
        tiles_ref[d, 0:5, 0:wide] = biases[:, d * wide : (d + 1) * wide]
        tiles_ref[d, 0:2, 32 : 32 + thin] = gains[:, d * thin : (d + 1) * thin]
        tiles_ref[d, 0:1, 64 : 64 + part] = to_gain[:, d * part : (d + 1) * part]
        tiles_ref[d, 0:part, 96 : 96 + heads] = to_weight[d * part : (d + 1) * part, :]


def finish_kernel(plan, orders, totals, sizes, *refs):
    tall, flat, long, small_at = sizes
    colors = len(orders)
    bits = len(orders[0])
    blocks = 1 << bits
    refs = list(refs)

    def take(count):
        out = refs[:count]
        del refs[:count]
        return out

    x_own_hbm, x_recv_hbm, g_own_hbm, g_send_hbm = take(4)
    small_refs = take(8)
    t_keep_a, t_keep_b, t_add_a, t_add_b = take(4)
    attn_ref, out_ref, cond_ref, small_ref, expand_ref, contract_ref = take(6)
    x_own, x_recv, g_own, g_recv, turned_ref, tiles_ref = take(6)
    parts = take(colors)
    landing = [take(bits) for _ in range(colors)]
    mine = take(colors)
    theirs = take(colors)
    t_mine, t_theirs = take(2), take(2)
    in_sems, send_sems, recv_sems = take(3)
    me = lax.axis_index("crop")
    side = lax.axis_index("seq")
    copies = fetch([(x_own_hbm, x_own), (x_recv_hbm, x_recv), (g_own_hbm, g_own)], in_sems)
    barrier = pltpu.get_barrier_semaphore()
    partners = [(flipped(me, 1 << bit), side) for bit in range(bits)] + [(me, 1 - side)]
    for partner in partners:
        pl.semaphore_signal(barrier, inc=1, device_id=partner, device_id_type=pl.DeviceIdType.MESH)
    pl.semaphore_wait(barrier, len(partners))
    used = [0]

    def ship(source, target, partner):
        k = used[0]
        used[0] += 1
        copy = pltpu.make_async_remote_copy(
            src_ref=source,
            dst_ref=target,
            send_sem=send_sems.at[k],
            recv_sem=recv_sems.at[k],
            device_id=partner,
            device_id_type=pl.DeviceIdType.MESH,
        )
        copy.start()
        return copy

    other_core = (me, 1 - side)
    across = ship(g_send_hbm, g_recv, other_core)
    for ref, keep, arrived in ((t_mine[0], t_keep_a, t_add_a), (t_mine[1], t_keep_b, t_add_b)):
        ref[...] = keep[0].astype(F32) + arrived[0].astype(F32)
    t_across = [ship(t_mine[k], t_theirs[k], other_core) for k in range(2)]
    small_tiles(tiles_ref, *small_refs)
    small_color, small_row = small_at
    for p in range(blocks):
        c = flipped(me, place(p, orders[small_color]))
        pair = tiles_ref[pl.ds(2 * c, 2)].astype(BF16)
        parts[small_color][p, small_row : small_row + 8, 0:128] = pair[0]
        parts[small_color][p, small_row : small_row + 8, 128:256] = pair[1]
        parts[small_color][p, small_row : small_row + 8, 256:384] = jnp.zeros((8, 128), BF16)
    copies[0].wait()
    copies[1].wait()

    flying = [[None] * bits for _ in range(colors)]

    def launch(color, j):
        count = blocks >> j
        bit = orders[color][j]
        partner = (flipped(me, 1 << bit), side)
        cuts = [(3 * count // 4, count), (count // 2, 3 * count // 4)] if count >= 4 else [(1, 2)]
        flying[color][j] = [
            (
                ship(
                    parts[color].at[low:high],
                    landing[color][j].at[low - count // 2 : high - count // 2],
                    partner,
                ),
                low - count // 2,
                high - count // 2,
            )
            for low, high in cuts
        ]

    last = [max(k for k, group in enumerate(plan) if any(use[1] == color for use in group[3])) for color in range(colors)]
    for k, (source, start, width, uses) in enumerate(plan):
        height = width // blocks
        if k == 0:
            copies[2].wait()
            across.wait()
        own, recv = ((x_own, x_recv), (g_own, g_recv))[source]
        span = slice(start, start + width)
        turned_ref[:width, :] = jnp.concatenate([own[:, span], recv[:, span]], axis=0).astype(F32).T
        for color in range(colors):
            wanted = [use for use in uses if use[1] == color]
            if wanted:
                left = jnp.concatenate(
                    [
                        turned_ref[pl.ds(flipped(me, place(p, orders[color])) * height, height), :]
                        for p in range(blocks)
                    ],
                    axis=0,
                ).astype(BF16)
            for column, _, offset in wanted:
                cut = slice(column, column + TILE)
                term = dot_nn(left, jnp.concatenate([g_own[:, cut], g_recv[:, cut]], axis=0)).astype(BF16)
                for p in range(blocks):
                    parts[color][p, offset : offset + height, :] = term[p * height : (p + 1) * height]
            if k == last[color]:
                launch(color, 0)

    def land(color, j, which):
        copy, low, high = flying[color][j][which]
        copy.wait()
        for p in range(low, high):
            both = parts[color][p].astype(F32) + landing[color][j][p].astype(F32)
            if j == bits - 1:
                mine[color][...] = both
            else:
                parts[color][p] = both.astype(BF16)

    for j in range(bits):
        for color in range(colors):
            land(color, j, 0)
            if j + 1 < bits:
                launch(color, j + 1)
        for color in range(colors):
            if len(flying[color][j]) > 1:
                land(color, j, 1)
        if j == 0:
            for copy in t_across:
                copy.wait()
            write_trans(tall, long, flat, side, t_mine, t_theirs, expand_ref, contract_ref, cond_ref)
    closing = [ship(mine[color], theirs[color], other_core) for color in range(colors)]
    for copy in closing:
        copy.wait()
    write_attn(tall, flat, side, mine, theirs, attn_ref, out_ref, cond_ref)
    ours = mine[small_color][small_row : small_row + 8, :]
    also = theirs[small_color][small_row : small_row + 8, :]
    both = ours + also
    small_ref[...] = jnp.where(side == 0, both[:, 0:128], both[:, 128:256])


def write_trans(tall, long, flat, side, mine, theirs, expand_ref, contract_ref, cond_ref):
    def unit(color, offset, height):
        return sides(side, mine[color], theirs[color], offset, height)

    for t in range(4):
        low, high = unit(0, t * tall, tall) if t < 3 else unit(1, 0, tall)
        expand_ref[:, 0, t * TILE : (t + 1) * TILE] = low
        expand_ref[:, 1, t * TILE : (t + 1) * TILE] = high
    low, high = unit(1, tall, long)
    contract_ref[:, :TILE] = low
    contract_ref[:, TILE:] = high
    low, high = unit(0, 3 * tall, flat)
    cond_ref[:, 3, :TILE] = low
    cond_ref[:, 4, :TILE] = high
    low, high = unit(1, tall + long, flat)
    cond_ref[:, 3, TILE:] = low
    cond_ref[:, 4, TILE:] = high
    low, high = unit(1, tall + long + flat, flat)
    cond_ref[:, 5, :TILE] = low
    cond_ref[:, 5, TILE:] = high


def write_attn(tall, flat, side, mine, theirs, attn_ref, out_ref, cond_ref):
    def unit(color, offset, height):
        return sides(side, mine[color], theirs[color], offset, height)

    spots = ((0, 0), (0, tall), (1, 0), (2, 0))
    for t, (color, offset) in enumerate(spots):
        low, high = unit(color, offset, tall)
        cut = slice((t % 2) * TILE, (t % 2 + 1) * TILE)
        attn_ref[:, t // 2, cut] = low
        attn_ref[:, 2 + t // 2, cut] = high
    low, high = unit(1, tall, tall)
    out_ref[:, :TILE] = low
    out_ref[:, TILE:] = high
    for t, (color, offset) in enumerate(((0, 2 * tall), (1, 2 * tall))):
        low, high = unit(color, offset, flat)
        cond_ref[:, 0, t * TILE : (t + 1) * TILE] = low
        cond_ref[:, 1, t * TILE : (t + 1) * TILE] = high
    low, high = unit(2, tall, flat)
    cond_ref[:, 2, :TILE] = low
    cond_ref[:, 2, TILE:] = high


def finish(crops, x_own, x_recv, g_own, g_send, small, state_t, arrived_t, sizes, first):
    tall, flat, long = sizes
    bits = crops.bit_length() - 1
    rows, width = x_own.shape[0], tall * crops
    cond_width, hidden_width = flat * crops, long * crops
    orders = (
        tuple(range(bits)),
        (1, 0) + tuple(range(2, bits)),
        tuple(range(2, bits)) + (0, 1),
    )
    c = [first + k * TILE for k in range(8)]
    plan = (
        (0, 0, width, ((c[0], 0, 0), (c[1], 0, tall), (c[2], 1, 0), (c[3], 2, 0))),
        (0, 2 * width, cond_width, ((c[5], 0, 2 * tall), (c[6], 1, 2 * tall))),
        (1, 0, width, ((c[4], 1, tall),)),
        (0, 2 * width + 2 * cond_width, cond_width, ((c[7], 2, tall),)),
    )
    totals = (2 * tall + flat, 2 * tall + flat + 8, tall + flat)
    small_at = (1, 2 * tall + flat)
    colors = len(orders)
    vm = pl.BlockSpec(memory_space=pltpu.VMEM)
    hbm = pl.BlockSpec(memory_space=pl.ANY)
    t_shapes = [keep.shape[1:] for keep, _ in state_t]
    ships = 1 + 2 + colors * (2 * (bits - 1) + 1) + colors
    devices = 2 * crops
    return pl.pallas_call(
        functools.partial(finish_kernel, plan, orders, totals, (tall, flat, long, small_at)),
        in_specs=[hbm] * 4 + [vm] * 12,
        out_specs=[vm] * 6,
        out_shape=[
            jax.ShapeDtypeStruct((tall // 2, 4, width), F32),
            jax.ShapeDtypeStruct((tall // 2, width), F32),
            jax.ShapeDtypeStruct((flat // 2, 6, width), F32),
            jax.ShapeDtypeStruct((8, 128), F32),
            jax.ShapeDtypeStruct((tall // 2, 2, hidden_width), F32),
            jax.ShapeDtypeStruct((long // 2, width), F32),
        ],
        scratch_shapes=[pltpu.VMEM(x_own.shape, BF16)] * 2
        + [pltpu.VMEM(g_own.shape, BF16)] * 2
        + [pltpu.VMEM((width, 2 * rows), F32), pltpu.VMEM((devices, 8, 128), F32)]
        + [pltpu.VMEM((crops, count, TILE), BF16) for count in totals]
        + [pltpu.VMEM((crops >> (j + 1), count, TILE), BF16) for count in totals for j in range(bits)]
        + [pltpu.VMEM((count, TILE), F32) for count in totals] * 2
        + [pltpu.VMEM(shape, F32) for shape in t_shapes] * 2
        + [
            pltpu.SemaphoreType.DMA((3,)),
            pltpu.SemaphoreType.DMA((ships,)),
            pltpu.SemaphoreType.DMA((ships,)),
        ],
        compiler_params=pltpu.CompilerParams(collective_id=1, has_side_effects=True),
        name="finish",
    )(
        x_own, x_recv, g_own, g_send, *small,
        state_t[0][0], state_t[1][0], arrived_t[0], arrived_t[1],
    )


def tie(*values):
    return lax.optimization_barrier(values)


def body(
    single,
    conditioning,
    pair_features,
    segments,
    pad_mask,
    cotangent,
    cond_gain,
    cond_weight,
    biases,
    attn_weight,
    out_weight,
    pair_gain,
    pair_weight,
    expand_weight,
    contract_weight,
):
    rows, width = single.shape
    cond_width = conditioning.shape[1]
    heads = pair_weight.shape[1]
    hidden_width = contract_weight.shape[0]
    crops = lax.axis_size("crop")
    bits = crops.bit_length() - 1
    me = lax.axis_index("crop").astype(jnp.int32).reshape(1)
    side = lax.axis_index("seq").astype(jnp.int32).reshape(1)
    orders = (tuple(range(bits)), (1, 0) + tuple(range(2, bits)))
    devices = 2 * crops
    chan_part = pair_gain.shape[0] // devices
    gains = cond_gain.T
    cond_weights = cond_weight.transpose(1, 0, 2)
    expand_weights = expand_weight.transpose(1, 0, 2)
    pair = pair_features[0]
    own_segments = lax.dynamic_slice(segments[0], (side[0] * rows,), (rows,))[:, None]

    x, scale0, keep0, own_t, send_t, kept, grad_norm1, grad_cond1, direct1, sums1, gain_sum1, w_forward, w_backward = trans(
        side, single, conditioning, cotangent, gains, biases.T, pair_gain[None], pair_weight.T,
        cond_weights, expand_weights, contract_weight,
    )
    x_other = swap(x)
    recv_t = swap(send_t)
    attn_weight, x = tie(attn_weight, x)
    attn_weights = attn_weight.transpose(1, 0, 2)
    attn_weights, x_other, recv_t = tie(attn_weights, x_other, recv_t)

    tall, flat, long = width // crops, cond_width // crops, hidden_width // crops
    low_at = 2 * width

    def columns(first):
        return [first + k * TILE for k in range(8)]

    c = columns(hidden_width)
    plan_t = (
        (0, width, width, ((c[0], 0, 0), (c[1], 0, tall), (c[2], 0, 2 * tall), (c[3], 1, 0))),
        (0, low_at + cond_width, cond_width, ((c[5], 0, 3 * tall), (c[6], 1, tall + long))),
        (1, 0, hidden_width, ((c[4], 1, tall),)),
        (0, low_at + 2 * cond_width, cond_width, ((c[7], 1, tall + long + flat),)),
    )
    totals_t = (3 * tall + flat, tall + long + 2 * flat)
    keep_a, send_a, keep_b, send_b = wgrad(me, x, x_other, own_t, recv_t, plan_t, orders, totals_t, "wgrad_trans")
    x, keep_a, send_a, keep_b, send_b = tie(x, keep_a, send_a, keep_b, send_b)
    state_t = [(keep_a, send_a), (keep_b, send_b)]
    arrived = arrivals(state_t, 0, orders)
    queries, kv, gate, grad_mixed, grad_attended = project(x, cotangent, biases.T, keep0, attn_weights, out_weight)
    kv_other = swap(kv)
    w_forward, grad_attended = tie(w_forward, grad_attended)
    bias, inv, mean = pair_fwd(pair, w_forward, heads)
    bias, kv_other, arrived = tie(bias, kv_other, arrived)
    state_t = added(state_t, arrived, "add_trans_0")
    bias, state_t = tie(bias, state_t)

    arrived = arrivals(state_t, 1, orders)
    attended, grad_queries, dkv_own, dkv_send, r, t, s = attention(
        side, queries, kv, kv_other, grad_attended, bias, inv, mean, own_segments, segments, pad_mask
    )
    dkv_send, arrived = tie(dkv_send, arrived)
    dkv_recv = swap(dkv_send)
    state_t = added(state_t, arrived, "add_trans_1")
    r, state_t = tie(r, state_t)

    arrived = arrivals(state_t, 2, orders)
    grad_pair, n_sum, c_sum = pair_bwd(pair, r, t, s, mean, w_backward)
    n_sum, dkv_recv, arrived = tie(n_sum, dkv_recv, arrived)
    state_t = added(state_t, arrived, "add_trans_2")
    dkv_recv, state_t = tie(dkv_recv, state_t)

    arrived = arrivals(state_t, 3, orders)
    own_a, sent_a, layer_out, grad_single, grad_cond, sums0, gain_sum0 = after(
        side, single, conditioning, cotangent, gains, attended, gate, out_weight, keep0, kept, grad_queries,
        dkv_own, dkv_recv, grad_mixed, attn_weights, scale0, cond_weights, grad_norm1, grad_cond1, direct1,
    )
    own_a, sent_a, arrived = tie(own_a, sent_a, arrived)
    for j in range(4, bits):
        state_t = added(state_t, arrived, "add_trans_" + str(j - 1))
        arrived = arrivals(state_t, j, orders)
    small_operands = (sums0, sums1, gain_sum0, gain_sum1, n_sum, c_sum, pair_gain[None], pair_weight.T)

    def results(attn, out, cond, small, expand, contract):
        return (
            layer_out,
            grad_single,
            grad_cond,
            grad_pair[None],
            small[:2, 32 : 32 + cond_width // devices].T,
            cond,
            small[:5, : width // devices].T,
            attn,
            out,
            small[0, 64 : 64 + chan_part],
            small[:chan_part, 96 : 96 + heads],
            expand,
            contract,
        )

    if tall % 8 == 0 and flat % 8 == 0:
        return results(
            *finish(crops, x, x_other, own_a, sent_a, small_operands, state_t, arrived, (tall, flat, long), width)
        )

    recv_a = swap(sent_a)
    c = columns(width)
    plan_a = (
        (0, 0, width, ((c[0], 0, 0), (c[1], 0, tall), (c[2], 0, 2 * tall), (c[3], 1, 0))),
        (1, 0, width, ((c[4], 1, tall),)),
        (0, low_at, cond_width, ((c[5], 1, 2 * tall), (c[6], 1, 2 * tall + flat))),
        (0, low_at + 2 * cond_width, cond_width, ((c[7], 1, 2 * tall + 2 * flat),)),
    )
    totals_a = (3 * tall, 2 * tall + 3 * flat)
    keep_a, send_a, keep_b, send_b = wgrad(me, x, x_other, own_a, recv_a, plan_a, orders, totals_a, "wgrad_attn")
    state_a = [(keep_a, send_a), (keep_b, send_b)]
    arrived_a = arrivals(state_a, 0, orders)
    state_t = added(state_t, arrived, "add_trans_last")
    trans_a, trans_b = state_t[0][0], state_t[1][0]
    trans_ra, trans_rb = swap(trans_a), swap(trans_b)
    state_a = added(state_a, arrived_a, "add_attn_0")
    arrived_a = arrivals(state_a, 1, orders)
    groups = tuple(min(2, bits - k) for k in range(0, bits, 2))
    parts = small_sums(me, crops, groups, *small_operands)
    landed = spread(parts, 0)
    trans_a, landed = tie(trans_a, landed)
    grad_expand, grad_contract, cond1 = close(
        functools.partial(close_trans_kernel, tall, long, flat),
        side,
        (trans_a, trans_b, trans_ra, trans_rb),
        ((tall // 2, 2, hidden_width), (long // 2, width), (3, flat // 2, width)),
        "close_trans",
    )
    shift = 0
    for j in range(1, bits):
        small_keep = parts[0]
        for v in landed:
            small_keep = small_keep + v
        cond1, small_keep, arrived_a = tie(cond1, small_keep, arrived_a)
        state_a = added(state_a, arrived_a, "add_attn_" + str(j))
        state_a, small_keep = tie(state_a, small_keep)
        if j + 1 < bits:
            arrived_a = arrivals(state_a, j + 1, orders)
        if j < len(groups):
            shift += groups[j - 1]
            step = 1 << groups[j]
            stacked = small_keep.reshape((-1, step) + small_keep.shape[1:])
            parts = [stacked[:, m] for m in range(step)]
            landed = spread(parts, shift)
        else:
            parts, landed = [small_keep], []
            if j == len(groups):
                small = small_keep[0]
                mine = jnp.where(side[0] == 0, small[0], small[1])
                small = mine + swap(jnp.where(side[0] == 0, small[1], small[0]))
                parts = [small]
    attn_a, attn_b = state_a[0][0], state_a[1][0]
    attn_ra, attn_rb = swap(attn_a), swap(attn_b)
    small = small_keep
    grad_attn_weight, grad_out, grad_cond_weight = close(
        functools.partial(close_attn_kernel, tall, flat),
        side,
        (attn_a, attn_b, attn_ra, attn_rb, cond1),
        ((tall // 2, 4, width), (tall // 2, width), (flat // 2, 6, width)),
        "close_attn",
    )
    return results(grad_attn_weight, grad_out, grad_cond_weight, small, grad_expand, grad_contract)


def solution(mesh):
    token = P(("crop", "seq"), None)
    whole = P()
    cube = P(("crop", "seq"), None, None)
    return jax.shard_map(
        body,
        mesh=mesh,
        in_specs=(token, token, P("crop", "seq", None, None), P("crop", None), P("crop", None), token)
        + (whole,) * 9,
        out_specs=(
            token, token, token, P("crop", "seq", None, None), token, cube, token, cube, token,
            P(("crop", "seq")), token, cube, token,
        ),
        check_vma=False,
    )
```

profile of v0, /device:TPU:0, one launch (start us, length us, event | category | flops | bytes accessed | tf_op | source)
XLA Modules:
  0.0 193.2 jit_solution(11842263735325870877)
XLA Ops:
  0.6 5.3 %copy.36 = bf16[768,2,1536]{2,0,1:T(8,128)(2,1)} copy(bf16[768,2,1536]{2,1,0:T(2,128)(2,1)} %param.28) | data formatting | bytes 9437184 | tf_op args[13]
  5.9 14.2 %trans.1 = (bf16[160,2688]{1,0:T(8,128)(2,1)}, f32[160,768]{1,0:T(8,128)}, f32[160,768]{1,0:T(8,128)}, bf16[160,4608]{1,0:T(8,128)(2,1)}, bf16[160,4608]{1,0:T(8...) custom-call(s32[1]{0:T(128)} %bitcast.side_ref.half_ref, ...), custom_call_target="tpu_custom_call" | custom-call | bytes 52428800 | tf_op jit(solution)/shard_map/trans/pallas_call | solution.py:403
  20.1 0.6 collective-permute-start.1
  20.7 0.1 collective-permute-start
  20.7 5.1 %copy.35 = bf16[768,4,768]{2,0,1:T(8,128)(2,1)} copy(bf16[768,4,768]{2,1,0:T(4,128)(2,1)} %param.24) | data formatting | bytes 9437184 | tf_op jit(solution)/shard_map/optimization_barrier | solution.py:1151
  25.8 0.0 collective-permute-done.refs_1_
  25.8 0.0 collective-permute-done.1.refs_3_
  25.8 0.0 copy-start.6
  25.8 0.9 copy-done.2
  26.7 0.5 copy-done.6
  27.2 7.6 %wgrad_trans.1 = (bf16[8,168,384]{2,1,0:T(8,128)(2,1)}, bf16[8,168,384]{2,1,0:T(8,128)(2,1)}, bf16[8,192,384]{2,1,0:T(8,128)(2,1)}, bf16[8,192,384]{2,1,0:T(8,128)(2,1)}) custom-call(s32[1]{0:T(128)} %bitcast.7.me_ref, bf16[160,2688]{1,0:T(8,128)(2,1)} %get-tuple-element.126.refs_0_.x_hbm, bf16[160,2688]{1,0:T(8,128)(2,1)} %copy-done.2, ...), custom_call_target="tpu_custom_call" | custom-call | bytes 27262976 | tf_op jit(solution)/shard_map/wgrad_trans/pallas_call | solution.py:682
  34.8 3.0 %collective-permute-start.4 = (bf16[8,192,384]{2,1,0:T(8,128)(2,1)}, bf16[8,192,384]{2,1,0:T(8,128)(2,1)S(1)}, u32[]{:S(2)}, u32[]{:S(2)}) collective-permute-start(bf16[8,192,384]{2,1,0:T(8,128)(2,1)} %get-tuple-element.136), channel_id=1, source_target_pairs={{0,4},{2,6},{4,0},{6,2},{8,12},{10,14},{12,8},{14,10},{16,20},{18,... | collective-permute-start | bytes 3538952 | tf_op jit(solution)/shard_map/ppermute | solution.py:716
  37.8 1.5 collective-permute-start.3
  39.3 5.6 %project.1 = (bf16[160,768]{1,0:T(8,128)(2,1)}, bf16[160,1536]{1,0:T(8,128)(2,1)}, f32[160,768]{1,0:T(8,128)}, f32[160,768]{1,0:T(8,128)}, bf16[160,768]{1,0:T(8,128)(2,1)}) custom-call(bf16[160,2688]{1,0:T(8,128)(2,1)} %get-tuple-element.126.refs_0_.x_hbm, bf16[160,768]{1,0:T(8,128)(2,1)} %cot_ref.5, bf16[5,768]{1,0:T(8,128)(2,1)} %bitcast.31, ...), custom_call_target="tpu_custom_call" | custom-call | bytes 23068672 | tf_op jit(solution)/shard_map/project/pallas_call | solution.py:492
  44.9 0.1 collective-permute-start.2
  44.9 13.2 %pair_fwd.1 = (bf16[16,160,320]{2,1,0:T(8,128)(2,1)}, f32[160,320]{1,0:T(8,128)}, f32[160,320]{1,0:T(8,128)}) custom-call(bf16[160,320,128]{2,1,0:T(8,128)(2,1)} %bitcast.23, bf16[64,128]{1,0:T(8,128)(2,1)} %get-tuple-element.133.w_ref), custom_call_target="tpu_custom_call" | custom-call | bytes 100663296 | tf_op jit(solution)/shard_map/pair_fwd/pallas_call | solution.py:65
  58.1 0.0 collective-permute-done.2.kr_ref.vr_ref
  58.1 4.4 %collective-permute-done.3.refs_2_.refs_3_ = bf16[8,168,384]{2,1,0:T(8,128)(2,1)S(1)} collective-permute-done((bf16[8,168,384]{2,1,0:T(8,128)(2,1)}, bf16[8,168,384]{2,1,0:T(8,128)(2,1)S(1)}, u32[]{:S(2)}, u32[]{:S(2)}) %collective-permute-start.3) | collective-permute-done | bytes 1032224 | tf_op jit(solution)/shard_map/ppermute | solution.py:716
  62.5 1.7 collective-permute-done.4.refs_6_.refs_7_
  64.2 0.0 copy-done.1
  64.2 1.0 copy-done
  65.2 4.4 %add_trans_0.1 = (bf16[4,168,384]{2,1,0:T(8,128)(2,1)}, bf16[4,168,384]{2,1,0:T(8,128)(2,1)}, bf16[4,192,384]{2,1,0:T(8,128)(2,1)}, bf16[4,192,384]{2,1,0:T(8,128)(2,1)}) custom-call(bf16[8,168,384]{2,1,0:T(8,128)(2,1)} %get-tuple-element.140.refs_0_.refs_1_, bf16[8,168,384]{2,1,0:T(8,128)(2,1)} %get-tuple-element.140.refs_0_.refs_1_, ...), custom_call_target="tpu_custom_call" | custom-call | bytes 2097152 | tf_op jit(solution)/shard_map/add_trans_0/pallas_call | solution.py:753
  69.6 1.8 collective-permute-start.6
  71.4 1.5 collective-permute-start.5
  72.9 0.1 dynamic-slice_bitcast_fusion
  73.0 0.8 copy.32.segc_ref
  73.7 17.4 %attn.1 = (bf16[160,768]{1,0:T(8,128)(2,1)}, bf16[160,768]{1,0:T(8,128)(2,1)}, f32[2,160,768]{2,1,0:T(8,128)}, f32[2,160,768]{2,1,0:T(8,128)}, bf16[16,160,320]{...) custom-call(s32[1]{0:T(128)} %bitcast.side_ref.half_ref, bf16[160,768]{1,0:T(8,128)(2,1)} %get-tuple-element.129.q_ref, ...), custom_call_target="tpu_custom_call" | custom-call | bytes 62914560 | tf_op jit(solution)/shard_map/attn/pallas_call | solution.py:165
  91.1 0.0 collective-permute-done.5.refs_2_.refs_3_
  91.2 0.0 collective-permute-done.6.refs_6_.refs_7_
  91.2 0.0 copy-start.3
  91.2 0.1 collective-permute-start.7
  91.3 0.7 copy-done.4
  92.0 0.2 copy-done.3
  92.1 2.5 %add_trans_1.1 = (bf16[2,168,384]{2,1,0:T(8,128)(2,1)}, bf16[2,168,384]{2,1,0:T(8,128)(2,1)}, bf16[2,192,384]{2,1,0:T(8,128)(2,1)}, bf16[2,192,384]{2,1,0:T(8,128)(2,1)}) custom-call(bf16[4,168,384]{2,1,0:T(8,128)(2,1)} %get-tuple-element.157.refs_0_.refs_1_, bf16[4,168,384]{2,1,0:T(8,128)(2,1)} %get-tuple-element.157.refs_0_.refs_1_, ...), custom_call_target="tpu_custom_call" | custom-call | bytes 2097152 | tf_op jit(solution)/shard_map/add_trans_1/pallas_call | solution.py:753
  94.7 1.6 collective-permute-start.9
  96.3 0.5 collective-permute-start.8
  96.7 14.4 %pair_bwd.1 = (bf16[160,320,128]{2,1,0:T(8,128)(2,1)}, f32[16,128]{1,0:T(8,128)}, f32[16,320]{1,0:T(8,128)}) custom-call(bf16[160,320,128]{2,1,0:T(8,128)(2,1)} %bitcast.24, bf16[16,160,320]{2,1,0:T(8,128)(2,1)} %get-tuple-element.168.r_ref, f32[160,320]{1,0:T(8,128)} %get-tuple-element.169.t_ref, f32[160,320]{1,0:T(8,128)} %get-tuple-element.170.s_ref, ...), custom_call_target="tpu_custom_call" | custom-call | bytes 62914560 | tf_op jit(solution)/shard_map/pair_bwd/pallas_call | solution.py:232
  111.2 0.0 collective-permute-done.8.refs_2_.refs_3_
  111.2 0.0 copy-start.8
  111.2 0.0 collective-permute-done.9.refs_6_.refs_7_
  111.2 0.0 copy-start.7
  111.2 0.0 collective-permute-done.7.dkv_recv_hbm
  111.2 0.0 copy-start.9
  111.2 0.6 copy-done.8
  111.9 0.1 copy-done.7
  112.0 2.1 %add_trans_2.1 = (bf16[1,168,384]{2,1,0:T(8,128)(2,1)}, bf16[1,168,384]{2,1,0:T(8,128)(2,1)}, bf16[1,192,384]{2,1,0:T(8,128)(2,1)}, bf16[1,192,384]{2,1,0:T(8,128)(2,1)}) custom-call(bf16[2,168,384]{2,1,0:T(8,128)(2,1)} %get-tuple-element.177.refs_0_.refs_1_, bf16[2,168,384]{2,1,0:T(8,128)(2,1)} %get-tuple-element.177.refs_0_.refs_1_, ...), custom_call_target="tpu_custom_call" | custom-call | bytes 2097152 | tf_op jit(solution)/shard_map/add_trans_2/pallas_call | solution.py:753
  114.1 2.6 %collective-permute-start.11 = (bf16[1,192,384]{2,1,0:T(8,128)(2,1)}, bf16[1,192,384]{2,1,0:T(8,128)(2,1)S(1)}, u32[]{:S(2)}, u32[]{:S(2)}) collective-permute-start(bf16[1,192,384]{2,1,0:T(8,128)(2,1)} %get-tuple-element.198), channel_id=1, source_target_pairs={{0,16},{2,18},{4,20},{6,22},{8,24},{10,26},{12,28},{14,30},{16,0},... | collective-permute-start | bytes 442376 | tf_op jit(solution)/shard_map/ppermute | solution.py:716
  116.7 0.3 collective-permute-start.10
  117.0 0.0 copy-done.9
  117.0 10.3 %after.1 = (bf16[160,3840]{1,0:T(8,128)(2,1)}, bf16[160,3840]{1,0:T(8,128)(2,1)}, bf16[160,768]{1,0:T(8,128)(2,1)}, f32[160,768]{1,0:T(8,128)}, f32[160,384]{1,0...) custom-call(s32[1]{0:T(128)} %bitcast.side_ref.half_ref, bf16[160,768]{1,0:T(8,128)(2,1)} %single_ref.3, ...), custom_call_target="tpu_custom_call" | custom-call | bytes 41943040 | tf_op jit(solution)/shard_map/after/pallas_call | solution.py:593
  127.4 1.3 collective-permute-done.10.refs_14_
  128.7 0.0 collective-permute-done.11.refs_15_
  128.8 0.6 copy-done.12
  129.4 0.1 copy-done.10
  129.4 51.2 %finish.1 = (f32[24,4,768]{2,1,0:T(4,128)}, f32[24,768]{1,0:T(8,128)}, f32[12,6,768]{2,1,0:T(8,128)}, f32[8,128]{1,0:T(8,128)}, f32[24,2,1536]{2,1,0:T(2,128)}, /*index=5*/f32[48,768]{1,0:T(8,128)}) custom-call(bf16[160,2688]{1,0:T(8,128)(2,1)} %get-tuple-element.126.refs_0_.x_hbm, bf16[160,2688]{1,0:T(8,128)(2,1)} %copy-done.2, ...), custom_call_target="tpu_custom_call" | custom-call | tf_op jit(solution)/shard_map/finish/pallas_call | solution.py:1118
  180.7 1.3 slice_bitcast_fusion.2
  182.0 1.3 slice_bitcast_fusion.1
  183.3 1.3 slice.15
  184.6 1.3 slice_bitcast_fusion
  185.9 1.7 copy.42
  187.6 1.7 copy.43
  189.3 1.5 copy.44
  190.8 1.7 copy.45
  192.5 0.7 copy.46
  (12 shorter events, 0.0 us)
Async XLA Ops:
  20.1 5.8 %collective-permute-start.1 = (bf16[160,4608]{1,0:T(8,128)(2,1)}, bf16[160,4608]{1,0:T(8,128)(2,1)S(1)}, u32[]{:S(2)}, u32[]{:S(2)}) collective-permute-start(bf16[160,4608]{1,0:T(8,128)(2,1)} %get-tuple-element.118), channel_id=1, source_target_pairs={{0,1},{1,0},{2,3},{3,2},{4,5},{5,4},{6,7},{7,6},{8,9},{9,8},{10,11... | collective-permute-start | bytes 4423688 | tf_op jit(solution)/shard_map/ppermute | solution.py:766
  20.7 5.2 %collective-permute-start = (bf16[160,2688]{1,0:T(8,128)(2,1)}, bf16[160,2688]{1,0:T(8,128)(2,1)S(1)}, u32[]{:S(2)}, u32[]{:S(2)}) collective-permute-start(bf16[160,2688]{1,0:T(8,128)(2,1)} %get-tuple-element.126.refs_0_.x_hbm), channel_id=1, source_target_pairs={{0,1},{1,0},{2,3},{3,2},{4,5},{5,4},{6,7},{7,6},{8,9},{9,8},{10,11... | collective-permute-start | bytes 2580488 | tf_op jit(solution)/shard_map/ppermute | solution.py:766
  25.8 0.9 copy-start.2
  25.8 1.4 copy-start.6
  34.8 29.4 %collective-permute-start.4 = (bf16[8,192,384]{2,1,0:T(8,128)(2,1)}, bf16[8,192,384]{2,1,0:T(8,128)(2,1)S(1)}, u32[]{:S(2)}, u32[]{:S(2)}) collective-permute-start(bf16[8,192,384]{2,1,0:T(8,128)(2,1)} %get-tuple-element.136), channel_id=1, source_target_pairs={{0,4},{2,6},{4,0},{6,2},{8,12},{10,14},{12,8},{14,10},{16,20},{18,... | collective-permute-start | bytes 3538952 | tf_op jit(solution)/shard_map/ppermute | solution.py:716
  37.8 24.7 %collective-permute-start.3 = (bf16[8,168,384]{2,1,0:T(8,128)(2,1)}, bf16[8,168,384]{2,1,0:T(8,128)(2,1)S(1)}, u32[]{:S(2)}, u32[]{:S(2)}) collective-permute-start(bf16[8,168,384]{2,1,0:T(8,128)(2,1)} %get-tuple-element.135), channel_id=1, source_target_pairs={{0,2},{2,0},{4,6},{6,4},{8,10},{10,8},{12,14},{14,12},{16,18},{18,... | collective-permute-start | bytes 3096584 | tf_op jit(solution)/shard_map/ppermute | solution.py:716
  44.9 13.3 %collective-permute-start.2 = (bf16[160,1536]{1,0:T(8,128)(2,1)}, bf16[160,1536]{1,0:T(8,128)(2,1)S(1)}, u32[]{:S(2)}, u32[]{:S(2)}) collective-permute-start(bf16[160,1536]{1,0:T(8,128)(2,1)} %get-tuple-element.130.ko_ref.vo_ref), channel_id=1, source_target_pairs={{0,1},{1,0},{2,3},{3,2},{4,5},{5,4},{6,7},{7,6},{8,9},{9,8},{10,11... | collective-permute-start | bytes 1474568 | tf_op jit(solution)/shard_map/ppermute | solution.py:766
  58.1 15.6 %copy-start.5 = (bf16[160,1536]{1,0:T(8,128)(2,1)}, bf16[160,1536]{1,0:T(8,128)(2,1)S(1)}, u32[]{:S(2)}) copy-start(bf16[160,1536]{1,0:T(8,128)(2,1)S(1)} %collective-permute-done.2.kr_ref.vr_ref) | copy-start | bytes 1474564
  62.5 1.7 copy-start.1
  64.2 1.0 copy-start
  65.2 7.7 %copy-start.13 = (s32[1,320]{1,0:T(1,128)S(1)}, s32[1,320]{1,0:T(1,128)}, u32[]{:S(2)}) copy-start(s32[1,320]{1,0:T(1,128)} %segr_ref.1) | copy-start | bytes 3844
  69.6 21.6 %collective-permute-start.6 = (bf16[4,192,384]{2,1,0:T(8,128)(2,1)}, bf16[4,192,384]{2,1,0:T(8,128)(2,1)S(1)}, u32[]{:S(2)}, u32[]{:S(2)}) collective-permute-start(bf16[4,192,384]{2,1,0:T(8,128)(2,1)} %get-tuple-element.160), channel_id=1, source_target_pairs={{0,2},{2,0},{4,6},{6,4},{8,10},{10,8},{12,14},{14,12},{16,18},{18,... | collective-permute-start | bytes 1769480 | tf_op jit(solution)/shard_map/ppermute | solution.py:716
  71.4 19.8 %collective-permute-start.5 = (bf16[4,168,384]{2,1,0:T(8,128)(2,1)}, bf16[4,168,384]{2,1,0:T(8,128)(2,1)S(1)}, u32[]{:S(2)}, u32[]{:S(2)}) collective-permute-start(bf16[4,168,384]{2,1,0:T(8,128)(2,1)} %get-tuple-element.159), channel_id=1, source_target_pairs={{0,4},{2,6},{4,0},{6,2},{8,12},{10,14},{12,8},{14,10},{16,20},{18,... | collective-permute-start | bytes 1548296 | tf_op jit(solution)/shard_map/ppermute | solution.py:716
  91.2 0.8 copy-start.4
  91.2 1.0 copy-start.3
  91.2 20.0 %collective-permute-start.7 = (f32[2,160,768]{2,1,0:T(8,128)}, f32[2,160,768]{2,1,0:T(8,128)S(1)}, u32[]{:S(2)}, u32[]{:S(2)}) collective-permute-start(f32[2,160,768]{2,1,0:T(8,128)} %get-tuple-element.173), channel_id=1, source_target_pairs={{0,1},{1,0},{2,3},{3,2},{4,5},{5,4},{6,7},{7,6},{8,9},{9,8},{10,11... | collective-permute-start | bytes 2949128 | tf_op jit(solution)/shard_map/ppermute | solution.py:766
  94.7 16.5 %collective-permute-start.9 = (bf16[2,192,384]{2,1,0:T(8,128)(2,1)}, bf16[2,192,384]{2,1,0:T(8,128)(2,1)S(1)}, u32[]{:S(2)}, u32[]{:S(2)}) collective-permute-start(bf16[2,192,384]{2,1,0:T(8,128)(2,1)} %get-tuple-element.175), channel_id=1, source_target_pairs={{0,8},{2,10},{4,12},{6,14},{8,0},{10,2},{12,4},{14,6},{16,24},{18,... | collective-permute-start | bytes 884744 | tf_op jit(solution)/shard_map/ppermute | solution.py:716
  96.3 14.9 %collective-permute-start.8 = (bf16[2,168,384]{2,1,0:T(8,128)(2,1)}, bf16[2,168,384]{2,1,0:T(8,128)(2,1)S(1)}, u32[]{:S(2)}, u32[]{:S(2)}) collective-permute-start(bf16[2,168,384]{2,1,0:T(8,128)(2,1)} %get-tuple-element.174), channel_id=1, source_target_pairs={{0,8},{2,10},{4,12},{6,14},{8,0},{10,2},{12,4},{14,6},{16,24},{18,... | collective-permute-start | bytes 774152 | tf_op jit(solution)/shard_map/ppermute | solution.py:716
  111.2 0.7 copy-start.8
  111.2 0.8 copy-start.7
  111.2 5.8 %copy-start.9 = (f32[2,160,768]{2,1,0:T(8,128)}, f32[2,160,768]{2,1,0:T(8,128)S(1)}, u32[]{:S(2)}) copy-start(f32[2,160,768]{2,1,0:T(8,128)S(1)} %collective-permute-done.7.dkv_recv_hbm) | copy-start | bytes 2949124
  114.1 14.6 %collective-permute-start.11 = (bf16[1,192,384]{2,1,0:T(8,128)(2,1)}, bf16[1,192,384]{2,1,0:T(8,128)(2,1)S(1)}, u32[]{:S(2)}, u32[]{:S(2)}) collective-permute-start(bf16[1,192,384]{2,1,0:T(8,128)(2,1)} %get-tuple-element.198), channel_id=1, source_target_pairs={{0,16},{2,18},{4,20},{6,22},{8,24},{10,26},{12,28},{14,30},{16,0},... | collective-permute-start | bytes 442376 | tf_op jit(solution)/shard_map/ppermute | solution.py:716
  116.7 12.0 %collective-permute-start.10 = (bf16[1,168,384]{2,1,0:T(8,128)(2,1)}, bf16[1,168,384]{2,1,0:T(8,128)(2,1)S(1)}, u32[]{:S(2)}, u32[]{:S(2)}) collective-permute-start(bf16[1,168,384]{2,1,0:T(8,128)(2,1)} %get-tuple-element.197), channel_id=1, source_target_pairs={{0,16},{2,18},{4,20},{6,22},{8,24},{10,26},{12,28},{14,30},{16,0},... | collective-permute-start | bytes 387080 | tf_op jit(solution)/shard_map/ppermute | solution.py:716
  128.7 0.7 copy-start.12
  128.8 0.7 copy-start.10
  180.7 11.8 %copy-start.11 = (f32[48,768]{1,0:T(8,128)S(1)}, f32[48,768]{1,0:T(8,128)}, u32[]{:S(2)}) copy-start(f32[48,768]{1,0:T(8,128)} %get-tuple-element.242) | copy-start | bytes 442372
where the time goes:
time: 194 us; the launch traced here: 193 us
  Pallas kernels  143 us (74%)
  local copies, waits for them, and re-layouts  28.4 us (15%)
  starting transfers between devices  13.6 us (7%)
  waiting for transfers between devices  7.44 us (4%)
    pallas_call x1, Pallas kernels, finish(): pl.pallas_call(functools.partial(finish_kernel, plan, orders, totals, (ta...  51.2 us
    pallas_call x1, Pallas kernels, attention(): pl.pallas_call(attn_kernel, grid=(groups,), in_specs=[pl.BlockSpec(memory...  17.4 us
    unnamed x34, local copies, waits for them, and re-layouts  17.3 us
    pallas_call x1, Pallas kernels, pair_bwd(): pl.pallas_call(pair_bwd_kernel, grid=(rows // tile,), in_specs=[pl.BlockS...  14.4 us
    pallas_call x1, Pallas kernels, trans(): pl.pallas_call(trans_kernel, in_specs=[pl.BlockSpec(memory_space=pltpu.SM...  14.2 us
    pallas_call x1, Pallas kernels, pair_fwd(): pl.pallas_call(pair_fwd_kernel, grid=(rows // tile,), in_specs=[pl.BlockS...  13.2 us
    ppermute x8, starting transfers between devices, send_half(): lax.ppermute(value, 'crop', [(i, i ^ 1 << bit) for i in range(count)])  12.8 us
    pallas_call x1, Pallas kernels, after(): pl.pallas_call(after_kernel, in_specs=[pl.BlockSpec(memory_space=pltpu.SM...  10.3 us
  transfers between devices with their start and end apart: 12, of which 3 were waited for; matrix products, arithmetic and copies ran while one was open for 3% of the time, Pallas kernels for 33%

commit v1 on v0

--- a/solution.py
+++ b/solution.py
@@ -904,8 +904,8 @@
         tiles_ref[d, 0:part, 96 : 96 + heads] = to_weight[d * part : (d + 1) * part, :]
 
 
-def finish_kernel(plan, orders, totals, sizes, *refs):
-    tall, flat, long, small_at = sizes
+def finish_kernel(plan, orders, small_at, *refs):
+    small_color, small_row = small_at
     colors = len(orders)
     bits = len(orders[0])
     blocks = 1 << bits
@@ -919,13 +919,11 @@
     x_own_hbm, x_recv_hbm, g_own_hbm, g_send_hbm = take(4)
     small_refs = take(8)
     t_keep_a, t_keep_b, t_add_a, t_add_b = take(4)
-    attn_ref, out_ref, cond_ref, small_ref, expand_ref, contract_ref = take(6)
+    mine, theirs = take(colors), take(colors)
+    t_mine, t_theirs = take(2), take(2)
     x_own, x_recv, g_own, g_recv, turned_ref, tiles_ref = take(6)
     parts = take(colors)
     landing = [take(bits) for _ in range(colors)]
-    mine = take(colors)
-    theirs = take(colors)
-    t_mine, t_theirs = take(2), take(2)
     in_sems, send_sems, recv_sems = take(3)
     me = lax.axis_index("crop")
     side = lax.axis_index("seq")
@@ -957,7 +955,6 @@
         ref[...] = keep[0].astype(F32) + arrived[0].astype(F32)
     t_across = [ship(t_mine[k], t_theirs[k], other_core) for k in range(2)]
     small_tiles(tiles_ref, *small_refs)
-    small_color, small_row = small_at
     for p in range(blocks):
         c = flipped(me, place(p, orders[small_color]))
         pair = tiles_ref[pl.ds(2 * c, 2)].astype(BF16)
@@ -1032,18 +1029,9 @@
         for color in range(colors):
             if len(flying[color][j]) > 1:
                 land(color, j, 1)
-        if j == 0:
-            for copy in t_across:
-                copy.wait()
-            write_trans(tall, long, flat, side, t_mine, t_theirs, expand_ref, contract_ref, cond_ref)
     closing = [ship(mine[color], theirs[color], other_core) for color in range(colors)]
-    for copy in closing:
+    for copy in t_across + closing:
         copy.wait()
-    write_attn(tall, flat, side, mine, theirs, attn_ref, out_ref, cond_ref)
-    ours = mine[small_color][small_row : small_row + 8, :]
-    also = theirs[small_color][small_row : small_row + 8, :]
-    both = ours + also
-    small_ref[...] = jnp.where(side == 0, both[:, 0:128], both[:, 128:256])
 
 
 def write_trans(tall, long, flat, side, mine, theirs, expand_ref, contract_ref, cond_ref):
@@ -1090,7 +1078,24 @@
     cond_ref[:, 2, TILE:] = high
 
 
-def finish(crops, x_own, x_recv, g_own, g_send, small, state_t, arrived_t, sizes, first):
+def outputs_kernel(sizes, *refs):
+    tall, flat, long, small_at, heads = sizes
+    side_ref, m0, m1, m2, h0, h1, h2, tm0, tm1, th0, th1 = refs[:11]
+    attn_ref, out_ref, cond_ref, gain_ref, bias_ref, pair_gain_ref, pair_weight_ref, expand_ref, contract_ref = refs[11:]
+    side = side_ref[0]
+    mine, theirs = (m0, m1, m2), (h0, h1, h2)
+    write_trans(tall, long, flat, side, (tm0, tm1), (th0, th1), expand_ref, contract_ref, cond_ref)
+    write_attn(tall, flat, side, mine, theirs, attn_ref, out_ref, cond_ref)
+    color, row = small_at
+    both = mine[color][row : row + 8, :] + theirs[color][row : row + 8, :]
+    small = jnp.where(side == 0, both[:, 0:128], both[:, 128:256])
+    bias_ref[...] = small[:5, 0 : bias_ref.shape[1]]
+    gain_ref[...] = small[:2, 32 : 32 + gain_ref.shape[1]]
+    pair_gain_ref[...] = small[:1, 64 : 64 + pair_gain_ref.shape[1]]
+    pair_weight_ref[...] = small[: pair_weight_ref.shape[0], 96 : 96 + heads]
+
+
+def finish(crops, side, x_own, x_recv, g_own, g_send, small, state_t, arrived_t, sizes, first, heads, chan_part):
     tall, flat, long = sizes
     bits = crops.bit_length() - 1
     rows, width = x_own.shape[0], tall * crops
@@ -1113,27 +1118,19 @@
     vm = pl.BlockSpec(memory_space=pltpu.VMEM)
     hbm = pl.BlockSpec(memory_space=pl.ANY)
     t_shapes = [keep.shape[1:] for keep, _ in state_t]
+    shapes = [(count, TILE) for count in totals] * 2 + t_shapes * 2
     ships = 1 + 2 + colors * (2 * (bits - 1) + 1) + colors
     devices = 2 * crops
-    return pl.pallas_call(
-        functools.partial(finish_kernel, plan, orders, totals, (tall, flat, long, small_at)),
+    sums = pl.pallas_call(
+        functools.partial(finish_kernel, plan, orders, small_at),
         in_specs=[hbm] * 4 + [vm] * 12,
-        out_specs=[vm] * 6,
-        out_shape=[
-            jax.ShapeDtypeStruct((tall // 2, 4, width), F32),
-            jax.ShapeDtypeStruct((tall // 2, width), F32),
-            jax.ShapeDtypeStruct((flat // 2, 6, width), F32),
-            jax.ShapeDtypeStruct((8, 128), F32),
-            jax.ShapeDtypeStruct((tall // 2, 2, hidden_width), F32),
-            jax.ShapeDtypeStruct((long // 2, width), F32),
-        ],
+        out_specs=[vm] * len(shapes),
+        out_shape=[jax.ShapeDtypeStruct(shape, F32) for shape in shapes],
         scratch_shapes=[pltpu.VMEM(x_own.shape, BF16)] * 2
         + [pltpu.VMEM(g_own.shape, BF16)] * 2
         + [pltpu.VMEM((width, 2 * rows), F32), pltpu.VMEM((devices, 8, 128), F32)]
         + [pltpu.VMEM((crops, count, TILE), BF16) for count in totals]
         + [pltpu.VMEM((crops >> (j + 1), count, TILE), BF16) for count in totals for j in range(bits)]
-        + [pltpu.VMEM((count, TILE), F32) for count in totals] * 2
-        + [pltpu.VMEM(shape, F32) for shape in t_shapes] * 2
         + [
             pltpu.SemaphoreType.DMA((3,)),
             pltpu.SemaphoreType.DMA((ships,)),
@@ -1144,6 +1141,17 @@
     )(
         x_own, x_recv, g_own, g_send, *small,
         state_t[0][0], state_t[1][0], arrived_t[0], arrived_t[1],
+    )
+    return close(
+        functools.partial(outputs_kernel, (tall, flat, long, small_at, heads)),
+        side,
+        sums,
+        (
+            (tall // 2, 4, width), (tall // 2, width), (flat // 2, 6, width),
+            (2, cond_width // devices), (5, width // devices), (1, chan_part), (chan_part, heads),
+            (tall // 2, 2, hidden_width), (long // 2, width),
+        ),
+        "outputs",
     )
 
 
@@ -1247,26 +1255,18 @@
         arrived = arrivals(state_t, j, orders)
     small_operands = (sums0, sums1, gain_sum0, gain_sum1, n_sum, c_sum, pair_gain[None], pair_weight.T)
 
-    def results(attn, out, cond, small, expand, contract):
+    def results(attn, out, cond, gain, bias, to_gain, to_weight, expand, contract):
         return (
-            layer_out,
-            grad_single,
-            grad_cond,
-            grad_pair[None],
-            small[:2, 32 : 32 + cond_width // devices].T,
-            cond,
-            small[:5, : width // devices].T,
-            attn,
-            out,
-            small[0, 64 : 64 + chan_part],
-            small[:chan_part, 96 : 96 + heads],
-            expand,
-            contract,
+            layer_out, grad_single, grad_cond, grad_pair[None], gain.T, cond, bias.T, attn, out,
+            to_gain.reshape(-1), to_weight, expand, contract,
         )
 
     if tall % 8 == 0 and flat % 8 == 0:
         return results(
-            *finish(crops, x, x_other, own_a, sent_a, small_operands, state_t, arrived, (tall, flat, long), width)
+            *finish(
+                crops, side, x, x_other, own_a, sent_a, small_operands, state_t, arrived, (tall, flat, long), width,
+                heads, chan_part,
+            )
         )
 
     recv_a = swap(sent_a)
@@ -1330,7 +1330,11 @@
         ((tall // 2, 4, width), (tall // 2, width), (flat // 2, 6, width)),
         "close_attn",
     )
-    return results(grad_attn_weight, grad_out, grad_cond_weight, small, grad_expand, grad_contract)
+    return results(
+        grad_attn_weight, grad_out, grad_cond_weight, small[:2, 32 : 32 + cond_width // devices],
+        small[:5, : width // devices], small[0, 64 : 64 + chan_part], small[:chan_part, 96 : 96 + heads],
+        grad_expand, grad_contract,
+    )
 
 
 def solution(mesh):

time: 194 us -> 184 us (0.948)
  local copies, waits for them, and re-layouts: 28.4 us -> 15.9 us
  Pallas kernels: 143 us -> 146 us
    unnamed x34 -> x27, local copies, waits for them, and re-layouts: 17.3 us -> 10 us
    pallas_call x1 -> x2, Pallas kernels: 51.2 us -> 54.3 us  [the longest x1 51.6 us: finish(): pl.pallas_call(functools.partial(finish_kernel, plan, orders, small_at),...]
    transpose x2 -> x0, local copies, waits for them, and re-layouts: 2.57 us -> none  [the longest x1 1.31 us: results(): small[:2, 32:32 + cond_width // devices]]
  transfers between devices with their start and end apart: 12 -> 12, of which waited for: 3 -> 3; matrix products, arithmetic and copies ran while one was open for 3% -> 3% of each run, Pallas kernels for 33% -> 35%
where the time goes in v1:
time: 184 us
  Pallas kernels  146 us (79%)
  local copies, waits for them, and re-layouts  15.9 us (9%)
  starting transfers between devices  13.6 us (7%)
  waiting for transfers between devices  7.44 us (4%)
    pallas_call x1, Pallas kernels, finish(): pl.pallas_call(functools.partial(finish_kernel, plan, orders, small_at),...  51.6 us
    pallas_call x1, Pallas kernels, attention(): pl.pallas_call(attn_kernel, grid=(groups,), in_specs=[pl.BlockSpec(memory...  17.4 us
    pallas_call x1, Pallas kernels, pair_bwd(): pl.pallas_call(pair_bwd_kernel, grid=(rows // tile,), in_specs=[pl.BlockS...  14.4 us
    pallas_call x1, Pallas kernels, trans(): pl.pallas_call(trans_kernel, in_specs=[pl.BlockSpec(memory_space=pltpu.SM...  14.2 us
    pallas_call x1, Pallas kernels, pair_fwd(): pl.pallas_call(pair_fwd_kernel, grid=(rows // tile,), in_specs=[pl.BlockS...  13.2 us
    ppermute x8, starting transfers between devices, send_half(): lax.ppermute(value, 'crop', [(i, i ^ 1 << bit) for i in range(count)])  12.8 us
    pallas_call x1, Pallas kernels, after(): pl.pallas_call(after_kernel, in_specs=[pl.BlockSpec(memory_space=pltpu.SM...  10.3 us
    unnamed x27, local copies, waits for them, and re-layouts  10 us
  transfers between devices with their start and end apart: 12, of which 3 were waited for; matrix products, arithmetic and copies ran while one was open for 3% of the time, Pallas kernels for 35%

profile of v1, /device:TPU:0, one launch (start us, length us, event | category | flops | bytes accessed | tf_op | source)
XLA Modules:
  0.0 183.9 jit_solution(7244538763967758683)
XLA Ops:
  0.6 5.3 %copy.36 = bf16[768,2,1536]{2,0,1:T(8,128)(2,1)} copy(bf16[768,2,1536]{2,1,0:T(2,128)(2,1)} %param.28) | data formatting | bytes 9437184 | tf_op args[13]
  5.9 14.2 %trans.1 = (bf16[160,2688]{1,0:T(8,128)(2,1)}, f32[160,768]{1,0:T(8,128)}, f32[160,768]{1,0:T(8,128)}, bf16[160,4608]{1,0:T(8,128)(2,1)}, bf16[160,4608]{1,0:T(8...) custom-call(s32[1]{0:T(128)} %bitcast.side_ref.half_ref.refs_0_, ...), custom_call_target="tpu_custom_call" | custom-call | bytes 52428800 | tf_op jit(solution)/shard_map/trans/pallas_call | solution.py:403
  20.1 0.6 collective-permute-start.1
  20.7 0.1 collective-permute-start
  20.7 5.1 %copy.35 = bf16[768,4,768]{2,0,1:T(8,128)(2,1)} copy(bf16[768,4,768]{2,1,0:T(4,128)(2,1)} %param.24) | data formatting | bytes 9437184 | tf_op jit(solution)/shard_map/optimization_barrier | solution.py:1159
  25.8 0.0 collective-permute-done.refs_1_
  25.8 0.0 copy-start.2
  25.8 0.0 collective-permute-done.1.refs_3_
  25.8 0.0 copy-start.6
  25.8 0.9 copy-done.2
  26.7 0.5 copy-done.6
  27.2 7.6 %wgrad_trans.1 = (bf16[8,168,384]{2,1,0:T(8,128)(2,1)}, bf16[8,168,384]{2,1,0:T(8,128)(2,1)}, bf16[8,192,384]{2,1,0:T(8,128)(2,1)}, bf16[8,192,384]{2,1,0:T(8,128)(2,1)}) custom-call(s32[1]{0:T(128)} %bitcast.7.me_ref, bf16[160,2688]{1,0:T(8,128)(2,1)} %get-tuple-element.139.refs_0_.x_hbm, bf16[160,2688]{1,0:T(8,128)(2,1)} %copy-done.2, ...), custom_call_target="tpu_custom_call" | custom-call | bytes 27262976 | tf_op jit(solution)/shard_map/wgrad_trans/pallas_call | solution.py:682
  34.8 3.0 %collective-permute-start.4 = (bf16[8,192,384]{2,1,0:T(8,128)(2,1)}, bf16[8,192,384]{2,1,0:T(8,128)(2,1)S(1)}, u32[]{:S(2)}, u32[]{:S(2)}) collective-permute-start(bf16[8,192,384]{2,1,0:T(8,128)(2,1)} %get-tuple-element.149), channel_id=1, source_target_pairs={{0,4},{2,6},{4,0},{6,2},{8,12},{10,14},{12,8},{14,10},{16,20},{18,... | collective-permute-start | bytes 3538952 | tf_op jit(solution)/shard_map/ppermute | solution.py:716
  37.8 1.5 collective-permute-start.3
  39.3 5.6 %project.1 = (bf16[160,768]{1,0:T(8,128)(2,1)}, bf16[160,1536]{1,0:T(8,128)(2,1)}, f32[160,768]{1,0:T(8,128)}, f32[160,768]{1,0:T(8,128)}, bf16[160,768]{1,0:T(8,128)(2,1)}) custom-call(bf16[160,2688]{1,0:T(8,128)(2,1)} %get-tuple-element.139.refs_0_.x_hbm, bf16[160,768]{1,0:T(8,128)(2,1)} %cot_ref.5, bf16[5,768]{1,0:T(8,128)(2,1)} %bitcast.28, ...), custom_call_target="tpu_custom_call" | custom-call | bytes 23068672 | tf_op jit(solution)/shard_map/project/pallas_call | solution.py:492
  44.9 0.1 collective-permute-start.2
  44.9 13.2 %pair_fwd.1 = (bf16[16,160,320]{2,1,0:T(8,128)(2,1)}, f32[160,320]{1,0:T(8,128)}, f32[160,320]{1,0:T(8,128)}) custom-call(bf16[160,320,128]{2,1,0:T(8,128)(2,1)} %bitcast.20, bf16[64,128]{1,0:T(8,128)(2,1)} %get-tuple-element.146.w_ref), custom_call_target="tpu_custom_call" | custom-call | bytes 100663296 | tf_op jit(solution)/shard_map/pair_fwd/pallas_call | solution.py:65
  58.1 0.0 collective-permute-done.2.kr_ref.vr_ref
  58.1 0.0 copy-start.5
  58.1 4.4 %collective-permute-done.3.refs_2_.refs_3_ = bf16[8,168,384]{2,1,0:T(8,128)(2,1)S(1)} collective-permute-done((bf16[8,168,384]{2,1,0:T(8,128)(2,1)}, bf16[8,168,384]{2,1,0:T(8,128)(2,1)S(1)}, u32[]{:S(2)}, u32[]{:S(2)}) %collective-permute-start.3) | collective-permute-done | bytes 1032224 | tf_op jit(solution)/shard_map/ppermute | solution.py:716
  62.5 0.0 copy-start.1
  62.5 1.7 collective-permute-done.4.refs_6_.refs_7_
  64.2 0.0 copy-start
  64.2 0.0 copy-done.1
  64.2 1.0 copy-done
  65.2 0.0 copy-start.12
  65.2 4.4 %add_trans_0.1 = (bf16[4,168,384]{2,1,0:T(8,128)(2,1)}, bf16[4,168,384]{2,1,0:T(8,128)(2,1)}, bf16[4,192,384]{2,1,0:T(8,128)(2,1)}, bf16[4,192,384]{2,1,0:T(8,128)(2,1)}) custom-call(bf16[8,168,384]{2,1,0:T(8,128)(2,1)} %get-tuple-element.153.refs_0_.refs_1_, bf16[8,168,384]{2,1,0:T(8,128)(2,1)} %get-tuple-element.153.refs_0_.refs_1_, ...), custom_call_target="tpu_custom_call" | custom-call | bytes 2097152 | tf_op jit(solution)/shard_map/add_trans_0/pallas_call | solution.py:753
  69.6 1.8 collective-permute-start.6
  71.4 1.5 collective-permute-start.5
  72.9 0.0 copy-done.12
  72.9 0.1 dynamic-slice_bitcast_fusion
  73.0 0.8 copy.32.segc_ref
  73.7 0.0 copy-done.5
  73.7 17.4 %attn.1 = (bf16[160,768]{1,0:T(8,128)(2,1)}, bf16[160,768]{1,0:T(8,128)(2,1)}, f32[2,160,768]{2,1,0:T(8,128)}, f32[2,160,768]{2,1,0:T(8,128)}, bf16[16,160,320]{...) custom-call(s32[1]{0:T(128)} %bitcast.side_ref.half_ref.refs_0_, bf16[160,768]{1,0:T(8,128)(2,1)} %get-tuple-element.142.q_ref, ...), custom_call_target="tpu_custom_call" | custom-call | bytes 62914560 | tf_op jit(solution)/shard_map/attn/pallas_call | solution.py:165
  91.1 0.0 collective-permute-done.5.refs_2_.refs_3_
  91.2 0.0 copy-start.4
  91.2 0.0 collective-permute-done.6.refs_6_.refs_7_
  91.2 0.0 copy-start.3
  91.2 0.1 collective-permute-start.7
  91.3 0.7 copy-done.4
  92.0 0.2 copy-done.3
  92.1 2.5 %add_trans_1.1 = (bf16[2,168,384]{2,1,0:T(8,128)(2,1)}, bf16[2,168,384]{2,1,0:T(8,128)(2,1)}, bf16[2,192,384]{2,1,0:T(8,128)(2,1)}, bf16[2,192,384]{2,1,0:T(8,128)(2,1)}) custom-call(bf16[4,168,384]{2,1,0:T(8,128)(2,1)} %get-tuple-element.170.refs_0_.refs_1_, bf16[4,168,384]{2,1,0:T(8,128)(2,1)} %get-tuple-element.170.refs_0_.refs_1_, ...), custom_call_target="tpu_custom_call" | custom-call | bytes 2097152 | tf_op jit(solution)/shard_map/add_trans_1/pallas_call | solution.py:753
  94.7 1.6 collective-permute-start.9
  96.3 0.5 collective-permute-start.8
  96.7 14.4 %pair_bwd.1 = (bf16[160,320,128]{2,1,0:T(8,128)(2,1)}, f32[16,128]{1,0:T(8,128)}, f32[16,320]{1,0:T(8,128)}) custom-call(bf16[160,320,128]{2,1,0:T(8,128)(2,1)} %bitcast.21, bf16[16,160,320]{2,1,0:T(8,128)(2,1)} %get-tuple-element.181.r_ref, f32[160,320]{1,0:T(8,128)} %get-tuple-element.182.t_ref, f32[160,320]{1,0:T(8,128)} %get-tuple-element.183.s_ref, ...), custom_call_target="tpu_custom_call" | custom-call | bytes 62914560 | tf_op jit(solution)/shard_map/pair_bwd/pallas_call | solution.py:232
  111.2 0.0 collective-permute-done.8.refs_2_.refs_3_
  111.2 0.0 copy-start.8
  111.2 0.0 collective-permute-done.9.refs_6_.refs_7_
  111.2 0.0 copy-start.7
  111.2 0.0 collective-permute-done.7.dkv_recv_hbm
  111.2 0.0 copy-start.9
  111.2 0.6 copy-done.8
  111.9 0.1 copy-done.7
  112.0 2.1 %add_trans_2.1 = (bf16[1,168,384]{2,1,0:T(8,128)(2,1)}, bf16[1,168,384]{2,1,0:T(8,128)(2,1)}, bf16[1,192,384]{2,1,0:T(8,128)(2,1)}, bf16[1,192,384]{2,1,0:T(8,128)(2,1)}) custom-call(bf16[2,168,384]{2,1,0:T(8,128)(2,1)} %get-tuple-element.190.refs_0_.refs_1_, bf16[2,168,384]{2,1,0:T(8,128)(2,1)} %get-tuple-element.190.refs_0_.refs_1_, ...), custom_call_target="tpu_custom_call" | custom-call | bytes 2097152 | tf_op jit(solution)/shard_map/add_trans_2/pallas_call | solution.py:753
  114.1 2.6 %collective-permute-start.11 = (bf16[1,192,384]{2,1,0:T(8,128)(2,1)}, bf16[1,192,384]{2,1,0:T(8,128)(2,1)S(1)}, u32[]{:S(2)}, u32[]{:S(2)}) collective-permute-start(bf16[1,192,384]{2,1,0:T(8,128)(2,1)} %get-tuple-element.211), channel_id=1, source_target_pairs={{0,16},{2,18},{4,20},{6,22},{8,24},{10,26},{12,28},{14,30},{16,0},... | collective-permute-start | bytes 442376 | tf_op jit(solution)/shard_map/ppermute | solution.py:716
  116.7 0.3 collective-permute-start.10
  117.0 0.0 copy-done.9
  117.0 10.3 %after.1 = (bf16[160,3840]{1,0:T(8,128)(2,1)}, bf16[160,3840]{1,0:T(8,128)(2,1)}, bf16[160,768]{1,0:T(8,128)(2,1)}, f32[160,768]{1,0:T(8,128)}, f32[160,384]{1,0...) custom-call(s32[1]{0:T(128)} %bitcast.side_ref.half_ref.refs_0_, bf16[160,768]{1,0:T(8,128)(2,1)} %single_ref.3, ...), custom_call_target="tpu_custom_call" | custom-call | bytes 41943040 | tf_op jit(solution)/shard_map/after/pallas_call | solution.py:593
  127.4 1.3 collective-permute-done.10.refs_14_
  128.7 0.0 collective-permute-done.11.refs_15_
  128.8 0.6 copy-done.11
  129.4 0.1 copy-done.10
  129.4 51.6 %finish.1 = (f32[120,384]{1,0:T(8,128)}, f32[128,384]{1,0:T(8,128)}, f32[72,384]{1,0:T(8,128)}, f32[120,384]{1,0:T(8,128)}, f32[128,384]{1,0:T(8,128)}, /*index=...) custom-call(bf16[160,2688]{1,0:T(8,128)(2,1)} %get-tuple-element.139.refs_0, ...), custom_call_target="tpu_custom_call" | custom-call | tf_op jit(solution)/shard_map/finish/pallas_call | solution.py:1124
  181.0 2.7 %outputs.1 = (f32[24,4,768]{2,1,0:T(4,128)}, f32[24,768]{1,0:T(8,128)}, f32[12,6,768]{2,1,0:T(8,128)}, f32[2,12]{1,0:T(2,128)}, f32[5,24]{1,0:T(8,128)}, /*index...) custom-call(s32[1]{0:T(128)} %bitcast.side_ref.half_ref.refs_0_, ...), custom_call_target="tpu_custom_call" | custom-call | bytes 4194304 | tf_op jit(solution)/shard_map/outputs/pallas_call | solution.py:825
  (2 shorter events, 0.0 us)
Async XLA Ops:
  20.1 5.8 %collective-permute-start.1 = (bf16[160,4608]{1,0:T(8,128)(2,1)}, bf16[160,4608]{1,0:T(8,128)(2,1)S(1)}, u32[]{:S(2)}, u32[]{:S(2)}) collective-permute-start(bf16[160,4608]{1,0:T(8,128)(2,1)} %get-tuple-element.131), channel_id=1, source_target_pairs={{0,1},{1,0},{2,3},{3,2},{4,5},{5,4},{6,7},{7,6},{8,9},{9,8},{10,11... | collective-permute-start | bytes 4423688 | tf_op jit(solution)/shard_map/ppermute | solution.py:766
  20.7 5.2 %collective-permute-start = (bf16[160,2688]{1,0:T(8,128)(2,1)}, bf16[160,2688]{1,0:T(8,128)(2,1)S(1)}, u32[]{:S(2)}, u32[]{:S(2)}) collective-permute-start(bf16[160,2688]{1,0:T(8,128)(2,1)} %get-tuple-element.139.refs_0_.x_hbm), channel_id=1, source_target_pairs={{0,1},{1,0},{2,3},{3,2},{4,5},{5,4},{6,7},{7,6},{8,9},{9,8},{10,11... | collective-permute-start | bytes 2580488 | tf_op jit(solution)/shard_map/ppermute | solution.py:766
  25.8 0.9 copy-start.2
  25.8 1.4 copy-start.6
  34.8 29.4 %collective-permute-start.4 = (bf16[8,192,384]{2,1,0:T(8,128)(2,1)}, bf16[8,192,384]{2,1,0:T(8,128)(2,1)S(1)}, u32[]{:S(2)}, u32[]{:S(2)}) collective-permute-start(bf16[8,192,384]{2,1,0:T(8,128)(2,1)} %get-tuple-element.149), channel_id=1, source_target_pairs={{0,4},{2,6},{4,0},{6,2},{8,12},{10,14},{12,8},{14,10},{16,20},{18,... | collective-permute-start | bytes 3538952 | tf_op jit(solution)/shard_map/ppermute | solution.py:716
  37.8 24.7 %collective-permute-start.3 = (bf16[8,168,384]{2,1,0:T(8,128)(2,1)}, bf16[8,168,384]{2,1,0:T(8,128)(2,1)S(1)}, u32[]{:S(2)}, u32[]{:S(2)}) collective-permute-start(bf16[8,168,384]{2,1,0:T(8,128)(2,1)} %get-tuple-element.148), channel_id=1, source_target_pairs={{0,2},{2,0},{4,6},{6,4},{8,10},{10,8},{12,14},{14,12},{16,18},{18,... | collective-permute-start | bytes 3096584 | tf_op jit(solution)/shard_map/ppermute | solution.py:716
  44.9 13.3 %collective-permute-start.2 = (bf16[160,1536]{1,0:T(8,128)(2,1)}, bf16[160,1536]{1,0:T(8,128)(2,1)S(1)}, u32[]{:S(2)}, u32[]{:S(2)}) collective-permute-start(bf16[160,1536]{1,0:T(8,128)(2,1)} %get-tuple-element.143.ko_ref.vo_ref), channel_id=1, source_target_pairs={{0,1},{1,0},{2,3},{3,2},{4,5},{5,4},{6,7},{7,6},{8,9},{9,8},{10,11... | collective-permute-start | bytes 1474568 | tf_op jit(solution)/shard_map/ppermute | solution.py:766
  58.1 15.6 %copy-start.5 = (bf16[160,1536]{1,0:T(8,128)(2,1)}, bf16[160,1536]{1,0:T(8,128)(2,1)S(1)}, u32[]{:S(2)}) copy-start(bf16[160,1536]{1,0:T(8,128)(2,1)S(1)} %collective-permute-done.2.kr_ref.vr_ref) | copy-start | bytes 1474564
  62.5 1.7 copy-start.1
  64.2 1.0 copy-start
  65.2 7.7 %copy-start.12 = (s32[1,320]{1,0:T(1,128)S(1)}, s32[1,320]{1,0:T(1,128)}, u32[]{:S(2)}) copy-start(s32[1,320]{1,0:T(1,128)} %segr_ref.1) | copy-start | bytes 3844
  69.6 21.6 %collective-permute-start.6 = (bf16[4,192,384]{2,1,0:T(8,128)(2,1)}, bf16[4,192,384]{2,1,0:T(8,128)(2,1)S(1)}, u32[]{:S(2)}, u32[]{:S(2)}) collective-permute-start(bf16[4,192,384]{2,1,0:T(8,128)(2,1)} %get-tuple-element.173), channel_id=1, source_target_pairs={{0,2},{2,0},{4,6},{6,4},{8,10},{10,8},{12,14},{14,12},{16,18},{18,... | collective-permute-start | bytes 1769480 | tf_op jit(solution)/shard_map/ppermute | solution.py:716
  71.4 19.8 %collective-permute-start.5 = (bf16[4,168,384]{2,1,0:T(8,128)(2,1)}, bf16[4,168,384]{2,1,0:T(8,128)(2,1)S(1)}, u32[]{:S(2)}, u32[]{:S(2)}) collective-permute-start(bf16[4,168,384]{2,1,0:T(8,128)(2,1)} %get-tuple-element.172), channel_id=1, source_target_pairs={{0,4},{2,6},{4,0},{6,2},{8,12},{10,14},{12,8},{14,10},{16,20},{18,... | collective-permute-start | bytes 1548296 | tf_op jit(solution)/shard_map/ppermute | solution.py:716
  91.2 0.8 copy-start.4
  91.2 1.0 copy-start.3
  91.2 20.0 %collective-permute-start.7 = (f32[2,160,768]{2,1,0:T(8,128)}, f32[2,160,768]{2,1,0:T(8,128)S(1)}, u32[]{:S(2)}, u32[]{:S(2)}) collective-permute-start(f32[2,160,768]{2,1,0:T(8,128)} %get-tuple-element.186), channel_id=1, source_target_pairs={{0,1},{1,0},{2,3},{3,2},{4,5},{5,4},{6,7},{7,6},{8,9},{9,8},{10,11... | collective-permute-start | bytes 2949128 | tf_op jit(solution)/shard_map/ppermute | solution.py:766
  94.7 16.5 %collective-permute-start.9 = (bf16[2,192,384]{2,1,0:T(8,128)(2,1)}, bf16[2,192,384]{2,1,0:T(8,128)(2,1)S(1)}, u32[]{:S(2)}, u32[]{:S(2)}) collective-permute-start(bf16[2,192,384]{2,1,0:T(8,128)(2,1)} %get-tuple-element.188), channel_id=1, source_target_pairs={{0,8},{2,10},{4,12},{6,14},{8,0},{10,2},{12,4},{14,6},{16,24},{18,... | collective-permute-start | bytes 884744 | tf_op jit(solution)/shard_map/ppermute | solution.py:716
  96.3 14.9 %collective-permute-start.8 = (bf16[2,168,384]{2,1,0:T(8,128)(2,1)}, bf16[2,168,384]{2,1,0:T(8,128)(2,1)S(1)}, u32[]{:S(2)}, u32[]{:S(2)}) collective-permute-start(bf16[2,168,384]{2,1,0:T(8,128)(2,1)} %get-tuple-element.187), channel_id=1, source_target_pairs={{0,8},{2,10},{4,12},{6,14},{8,0},{10,2},{12,4},{14,6},{16,24},{18,... | collective-permute-start | bytes 774152 | tf_op jit(solution)/shard_map/ppermute | solution.py:716
  111.2 0.7 copy-start.8
  111.2 0.8 copy-start.7
  111.2 5.8 %copy-start.9 = (f32[2,160,768]{2,1,0:T(8,128)}, f32[2,160,768]{2,1,0:T(8,128)S(1)}, u32[]{:S(2)}) copy-start(f32[2,160,768]{2,1,0:T(8,128)S(1)} %collective-permute-done.7.dkv_recv_hbm) | copy-start | bytes 2949124
  114.1 14.6 %collective-permute-start.11 = (bf16[1,192,384]{2,1,0:T(8,128)(2,1)}, bf16[1,192,384]{2,1,0:T(8,128)(2,1)S(1)}, u32[]{:S(2)}, u32[]{:S(2)}) collective-permute-start(bf16[1,192,384]{2,1,0:T(8,128)(2,1)} %get-tuple-element.211), channel_id=1, source_target_pairs={{0,16},{2,18},{4,20},{6,22},{8,24},{10,26},{12,28},{14,30},{16,0},... | collective-permute-start | bytes 442376 | tf_op jit(solution)/shard_map/ppermute | solution.py:716
  116.7 12.0 %collective-permute-start.10 = (bf16[1,168,384]{2,1,0:T(8,128)(2,1)}, bf16[1,168,384]{2,1,0:T(8,128)(2,1)S(1)}, u32[]{:S(2)}, u32[]{:S(2)}) collective-permute-start(bf16[1,168,384]{2,1,0:T(8,128)(2,1)} %get-tuple-element.210), channel_id=1, source_target_pairs={{0,16},{2,18},{4,20},{6,22},{8,24},{10,26},{12,28},{14,30},{16,0},... | collective-permute-start | bytes 387080 | tf_op jit(solution)/shard_map/ppermute | solution.py:716
  128.7 0.7 copy-start.11
  128.8 0.7 copy-start.10
